TPU v7x, 256 devices: a whole 4x4x8 slice. The times are simulated.
256 devices in a mesh: row: 8 (over x, y_lo), col: 32 (over z, y_hi, core).
Axes of the slice: x: 4, y: 4 (y_hi: 2, y_lo: 2; y = y_hi * 2 + y_lo), z: 8, core: 2. Of those that a mesh axis runs over, the one named last changes fastest.
Arguments:
- ancestor_inverse: float32 [16384, 16384], P('row', 'col'), may hold values from -6 to 6
- panel: float32 [6, 64, 256, 256], P(None, 'row', 'col'), may hold values from -0.0625 to 0.0625
- diag_inverse: float32 [6, 256, 256], replicated, as said below
- structure: int32 [6, 32], replicated, may hold values from 0 to 63, as said below
- block_slot: int32 [64], replicated, may hold values from 0 to 63, as said below
Outputs:
- off_block: float32 [6, 64, 256, 256], P(None, 'row', 'col')
- diag_block: float32 [6, 256, 256], replicated
Inputs may be any that keep to these rules, and one draw needn't show every extreme that they name: `structure`: the 32 entries of a supernode are distinct global row blocks. Mapped through block_slot, at most 6 of them fall into any aligned run of 8 storage slots, and for every supernode some run holds exactly 6. `block_slot`: A permutation of the 64 row blocks. `diag_inverse`: lower triangular with a positive diagonal.
All inputs are finite; a program needn't handle non-finite values.
Results may differ from a plain program's by a relative error of at most 0.0001.
Values sent between devices are 32-bit elements; how exact they have to be, the bound alone decides.
A program may use at most 128 MiB of HBM per device.

v0:
```python
import jax
import jax.numpy as jnp
from jax import lax
from jax.sharding import PartitionSpec as P


def spread(block, axis, owner):
    block = jnp.where(lax.axis_index(axis) == owner, block, jnp.zeros_like(block))
    return lax.psum(block, axis)


def gather_rows(normalized):
    return lax.all_gather(normalized, "col", axis=2, tiled=True)


def body(ancestor_inverse, panel, diag_inverse, structure, block_slot):
    highest = lax.Precision.HIGHEST
    row_count = lax.axis_size("row")
    col_count = lax.axis_size("col")
    row_index = lax.axis_index("row")
    col_index = lax.axis_index("col")
    node_count, slot_count, sub_rows, block_width = panel.shape
    total_slots = slot_count * row_count
    col_slots = total_slots // col_count
    slot_range = jnp.arange(total_slots, dtype=jnp.int32)
    lookup = (structure[:, :, None] == slot_range[None, None, :]).astype(jnp.int32)
    slot_ids = jnp.sum(lookup * block_slot[None, None, :], axis=2)
    chosen = jnp.any(slot_ids[:, :, None] == slot_range[None, None, :], axis=1).astype(jnp.int32)
    local_mask = lax.dynamic_slice_in_dim(chosen, row_index * slot_count, slot_count, 1)
    weight_mask = local_mask.astype(jnp.float32)[:, :, None, None]
    normalized = jnp.einsum("sqik,skw->sqiw", panel, diag_inverse, precision=highest) * weight_mask
    first_slot = col_index * col_slots
    owner_row = first_slot // slot_count
    row_panel = gather_rows(normalized)
    picked = lax.dynamic_slice_in_dim(row_panel, first_slot % slot_count, col_slots, 1)
    column_panel = spread(picked, "row", owner_row)
    column_rows = column_panel.reshape(node_count, col_slots * block_width, block_width)
    leading = jnp.einsum("sij,sik->sjk", diag_inverse, diag_inverse, precision=highest)
    partial_value = jnp.einsum("rc,scw->srw", ancestor_inverse, column_rows, precision=highest)
    partial_value = partial_value.reshape(node_count, slot_count, block_width, block_width)
    product = lax.psum_scatter(partial_value, "col", scatter_dimension=2, tiled=True) * weight_mask
    diag_terms = jnp.einsum("saiw,saiv->swv", normalized, product, precision=highest)
    diag_sum = lax.psum(diag_terms, ("row", "col"))
    return (-product, leading + diag_sum)


def solution(mesh):
    in_specs = (P("row", "col"), P(None, "row", "col", None), P(), P(), P())
    out_specs = (P(None, "row", "col", None), P())
    return jax.shard_map(body, mesh=mesh, in_specs=in_specs, out_specs=out_specs, check_vma=False)
```

profile of v0, /device:TPU:1, one launch (start us, length us, event | category | flops | bytes accessed | tf_op | source)
XLA Modules:
  0.0 784.7 jit_solution(1780212181948259479)
XLA Ops:
  7.2 0.0 copy-start
  7.2 0.0 all-gather.2.cloned.1.call-start
  7.2 1.1 select_reduce_fusion
  8.3 0.1 fusion.8
  8.4 0.1 dynamic-slice_convert_fusion
  8.5 0.1 copy-done
  8.6 2.8 fusion.3
  11.4 0.0 all-gather.2.cloned.1.call-update
  11.5 0.0 all-reduce.3.cloned.1.call-start
  11.5 134.1 %all-gather.2.cloned.1.call-done = f32[6,8,256,256]{3,2,1,0:T(8,128)} async-done(((f32[6,8,8,256]{3,2,1,0:T(8,128)}), f32[6,8,256,256]{3,2,1,0:T(8,128)}) %all-gather.2.cloned.1.call-update) | async-done | bytes 12582928 | tf_op jit(solution)/shard_map/all_gather | solution.py:13
  145.6 3.8 dynamic-slice_select_fusion
  149.4 3.5 copy.10
  153.0 0.0 all-reduce.3.cloned.1.call-update
  153.0 0.0 reduce-scatter.2.cloned.1.call-start
  153.0 143.3 %all-reduce.3.cloned.1.call-done = f32[6,512,256]{1,2,0:T(8,128)} async-done(((f32[6,512,256]{1,2,0:T(8,128)}), f32[6,512,256]{1,2,0:T(8,128)}) %all-reduce.3.cloned.1.call-update) | async-done | bytes 3145744 | tf_op jit(solution)/shard_map/psum | solution.py:9
  296.3 24.8 %convolution_bitcast_fusion = f32[6,2048,256]{1,2,0:T(8,128)} fusion(f32[6,512,256]{1,2,0:T(8,128)} %all-reduce.3.cloned.1.call-done, f32[2048,512]{1,0:T(8,128)} %param.5), kind=kOutput, calls=%fused_computation | convolution fusion | flops 19327352832 | bytes 19922944 | tf_op jit(solution)/shard_map/rc,scw->srw/dot_general | solution.py:39
  321.1 12.6 %copy.11 = f32[6,2048,256]{2,1,0:T(8,128)} copy(f32[6,2048,256]{1,2,0:T(8,128)} %convolution_bitcast_fusion) | data formatting | bytes 25165824 | tf_op jit(solution)/shard_map/rc,scw->srw/transpose | solution.py:39
  333.7 0.0 copy-start.1
  333.7 0.0 reduce-scatter.2.cloned.1.call-update
  333.7 0.2 all-reduce.5.cloned.1.call-start
  333.9 170.3 %reduce-scatter.2.cloned.1.call-done = f32[6,8,8,256]{3,2,1,0:T(8,128)} async-done(((f32[6,8,256,256]{3,2,1,0:T(8,128)}), f32[6,8,8,256]{3,2,1,0:T(8,128)}) %reduce-scatter.2.cloned.1.call-update) | async-done | bytes 393232 | tf_op jit(solution)/shard_map/reduce_scatter | solution.py:41
  504.2 0.0 copy-done.1
  504.2 0.0 copy-start.2
  504.2 3.8 convolution_bitcast_fusion.1
  508.0 0.0 all-reduce.5.cloned.1.call-update
  508.0 0.0 copy-done.2
  508.0 0.9 multiply_negate_fusion
  508.9 264.1 %all-reduce.5.cloned.1.call-done = f32[6,256,256]{2,1,0:T(8,128)} async-done(((f32[6,256,256]{2,1,0:T(8,128)}), f32[6,256,256]{2,1,0:T(8,128)}) %all-reduce.5.cloned.1.call-update) | async-done | bytes 1572880 | tf_op jit(solution)/shard_map/psum | solution.py:43
  773.0 5.2 convolution_add_fusion
  (1 shorter events, 0.0 us)
Async XLA Ops:
  7.2 1.4 copy-start
  7.2 138.4 %all-gather.2.cloned.1.call-start = ((), (), s32[]{:S(2)}) async-start(), calls=%async_computation.1 | async-start | bytes 12976128 | tf_op jit(solution)/shard_map/all_gather | solution.py:13
  11.5 284.8 %all-reduce.3.cloned.1.call-start = ((), (), s32[]{:S(2)}) async-start(), calls=%async_computation.2 | async-start | bytes 6291456 | tf_op jit(solution)/shard_map/psum | solution.py:9
  153.0 351.2 %reduce-scatter.2.cloned.1.call-start = ((), (), s32[]{:S(2)}) async-start(), calls=%async_computation.3 | async-start | bytes 12976128 | tf_op jit(solution)/shard_map/reduce_scatter | solution.py:41
  333.7 170.5 %copy-start.1 = (f32[6,8,8,256]{3,2,1,0:T(8,128)S(1)}, f32[6,8,8,256]{3,2,1,0:T(8,128)}, u32[]{:S(2)}) copy-start(f32[6,8,8,256]{3,2,1,0:T(8,128)} %fusion.3) | copy-start | bytes 1179652
  333.7 439.3 %all-reduce.5.cloned.1.call-start = ((), (), s32[]{:S(2)}) async-start(), calls=%async_computation.4 | async-start | bytes 3145728 | tf_op jit(solution)/shard_map/psum | solution.py:43
  504.2 3.8 copy-start.2
Sparse Core Ops, SparseCore 0:
  11.6 133.9 all-gather.1
  153.1 143.1 all-reduce.2
  333.8 170.3 reduce-scatter.1
  510.0 262.9 all-reduce.4
where the time goes:
time: 786 us; the launch traced here: 785 us
  waiting for transfers between devices  712 us (91%)
  matrix products  36.6 us (5%)
  local copies, waits for them, and re-layouts  16.3 us (2%)
  between operations  13.8 us (2%)
    psum x1, waiting for transfers between devices, body(): diag_sum = lax.psum(diag_terms, ('row', 'col'))  264 us
    reduce_scatter x1, waiting for transfers between devices, body(): lax.psum_scatter(partial_value, 'col', scatter_dimension=2, tiled=True)  170 us
    psum x1, waiting for transfers between devices, spread(): return lax.psum(block, axis)  143 us
    all_gather x1, waiting for transfers between devices, gather_rows(): return lax.all_gather(normalized, 'col', axis=2, tiled=True)  134 us
    dot_general x1, matrix products, body(): jnp.einsum('rc,scw->srw', ancestor_inverse, column_rows, precision=highest)  24.8 us
  transfers between devices with their start and end apart: 4, of which 4 were waited for; matrix products, arithmetic and copies ran while one was open for 0% of the time, Pallas kernels for 0%

commit v1 on v0

v1 whole, which is shorter than its diff:
```python
import functools

import jax
import jax.numpy as jnp
from jax import lax
from jax.experimental import pallas as pl
from jax.experimental.pallas import tpu as pltpu
from jax.sharding import PartitionSpec as P

F32 = jnp.float32
BF16 = jnp.bfloat16
MESH = pl.DeviceIdType.MESH
HIGHEST = lax.Precision.HIGHEST

NR = 8
NZ = 8
CAP = 6
LAG = 4


def halves(value):
    high = value.astype(BF16)
    return high, (value - high.astype(F32)).astype(BF16)


def wait_for(ref, sem):
    pltpu.make_async_copy(ref, ref, sem).wait()


def kernel(
    group,
    ids, pos, mask, a_ref, panel, dinv, off, diag,
    af, ahi, alo, nsrc, nflat, abuf, nbuf, nhi, nlo, ybuf, rbuf, pbuf, yfin,
    dbuf, drow, ebuf, ez, fq, gr, lead,
    a_sem, s1_s, s1_r, s1_l, s2_s, s2_r, s2_l,
    c1_s, c1_r, c2_s, c2_r, c3_s, c3_r, sh_s, sh_r,
    ring_s, ring_r, p_s, p_r, d_s, d_r,
):
    nodes, slots, sub, width = panel.shape
    lane = width // 2
    groups = nodes // group
    r = lax.axis_index("row")
    c = lax.axis_index("col")
    z = c // 4
    yh = lax.rem(c // 2, 2)
    core = lax.rem(c, 2)
    q = lax.rem(c, 4)
    zy = c // 2
    x = r // 2
    yl = lax.rem(r, 2)

    def dev(row, zz, qq):
        return {"row": row, "col": zz * 4 + qq}

    def send(src, dst, ssem, rsem, where):
        pltpu.make_async_remote_copy(
            src_ref=src, dst_ref=dst, send_sem=ssem, recv_sem=rsem,
            device_id=where, device_id_type=MESH,
        ).start()

    mate = dev(r, z, yh * 2 + 1 - core)
    across = dev(r, z, (1 - yh) * 2 + core)

    def row_peer(i):
        return lax.rem(r + i, NR)

    def zy_peer(i):
        return lax.rem(zy + i, 2 * NZ)

    def z_peer(i):
        return lax.rem(z + i, NZ)

    own_a = pltpu.make_async_copy(a_ref.at[:, :, core], af.at[core], a_sem.at[0])
    own_a.start()

    barrier = pltpu.get_barrier_semaphore()

    def greet(where):
        pl.semaphore_signal(barrier, inc=1, device_id=where, device_id_type=MESH)

    @pl.loop(1, NR)
    def _(i):
        greet({"row": row_peer(i), "col": c})

    @pl.loop(1, 2 * NZ)
    def _(i):
        greet({"row": r, "col": zy_peer(i) * 2 + core})

    greet(mate)
    greet(dev(r, z, 3 - q))

    @pl.loop(0, nodes)
    def _(s):
        value = jnp.dot(
            panel[s].reshape(slots * sub, width), dinv[s],
            precision=HIGHEST, preferred_element_type=F32,
        )
        for k in range(slots):
            part = value[k * sub:(k + 1) * sub] * mask[s, k].astype(F32)
            nflat[s, k * sub:(k + 1) * sub, :] = part
            for h in range(2):
                nsrc[s, k // 4, (k % 4) * 2 + h] = part[:, h * lane:(h + 1) * lane]

    pl.semaphore_wait(barrier, NR - 1 + 2 * NZ - 1 + 2)

    for g in range(groups):
        span = pl.ds(g * group, group)
        pltpu.make_async_copy(nsrc.at[span, :, r], abuf.at[g, r], s1_l.at[g]).start()

        @pl.loop(1, NR)
        def _(i):
            p = row_peer(i)
            send(nsrc.at[span, :, p], abuf.at[g, r], s1_s.at[g], s1_r.at[g], {"row": p, "col": c})

    send(a_ref.at[:, :, 1 - core], af.at[core], a_sem.at[1], a_sem.at[2], mate)

    for g in range(groups):
        span = pl.ds(g * group, group)
        wait_for(abuf.at[g, r], s1_l.at[g])
        wait_for(abuf.at[g, pl.ds(0, NR - 1)], s1_r.at[g])
        pltpu.make_async_copy(abuf.at[g, z, :, yh], nbuf.at[span, r, zy, core], s2_l.at[g]).start()

        @pl.loop(1, 2 * NZ)
        def _(i):
            t = zy_peer(i)
            send(
                abuf.at[g, t // 2, :, lax.rem(t, 2)], nbuf.at[span, r, zy, core],
                s2_s.at[g], s2_r.at[g], {"row": r, "col": t * 2 + core},
            )

    @pl.loop(0, nodes)
    def _(s):
        lead[s] = lax.dot_general(
            dinv[s], dinv[s], (((0,), (0,)), ((), ())),
            precision=HIGHEST, preferred_element_type=F32,
        )

    own_a.wait()
    wait_for(af.at[1 - core], a_sem.at[2])

    @pl.loop(0, slots)
    def _(k):
        for h in range(2):
            rows, cols = ahi.shape[1], ahi.shape[2] // 2
            high, low = halves(af[h, k].reshape(rows, cols))
            ahi[k, :, h * cols:(h + 1) * cols] = high
            alo[k, :, h * cols:(h + 1) * cols] = low

    right = {"row": lax.rem(x + 1, 4) * 2 + yl, "col": c}
    left = {"row": lax.rem(x + 3, 4) * 2 + yl, "col": c}
    twin = {"row": x * 2 + 1 - yl, "col": c}
    xl, xr, xo = lax.rem(x + 3, 4), lax.rem(x + 1, 4), lax.rem(x + 2, 4)
    way = 1 - 2 * core
    onward = dev(lax.rem(r, NR), lax.rem(z + way + NZ, NZ), q)

    def block(s, p):
        return nbuf.at[s, p, :, core]

    def relay_one(s):
        @pl.when(lax.rem(s, group) == 0)
        def _():
            g = s // group
            wait_for(nbuf.at[pl.ds(0, group), r, zy, core], s2_l.at[g])
            wait_for(nbuf.at[pl.ds(0, group), r, pl.ds(0, 2 * NZ - 1), core], s2_r.at[g])
        send(block(s, r), block(s, r), c1_s.at[s], c1_r.at[s], twin)

    def relay_two(s):
        wait_for(block(s, r), c1_r.at[s])
        pair = nbuf.at[s, pl.ds(2 * x, 2), :, core]
        send(pair, pair, c2_s.at[s, 0], c2_r.at[s, 0], right)
        send(pair, pair, c2_s.at[s, 1], c2_r.at[s, 1], left)

    def relay_three(s):
        wait_for(nbuf.at[s, pl.ds(0, 2), :, core], c2_r.at[s, 0])
        send(block(s, 2 * xl), block(s, 2 * xl), c3_s.at[s, 0], c3_r.at[s, 0], right)
        wait_for(nbuf.at[s, pl.ds(0, 2), :, core], c2_r.at[s, 1])
        send(block(s, 2 * xr + 1), block(s, 2 * xr + 1), c3_s.at[s, 1], c3_r.at[s, 1], left)

    def share(s):
        wait_for(block(s, 2 * xo), c3_r.at[s, 0])
        wait_for(block(s, 2 * xo + 1), c3_r.at[s, 1])
        mine = nbuf.at[s, :, :, core]
        send(mine, mine, sh_s.at[s], sh_r.at[s], mate)

    def multiply(s):
        wait_for(nbuf.at[s, :, :, 1 - core], sh_r.at[s])
        for j in range(4):
            for h in range(2):
                high, low = halves(nbuf[s, 2 * j + h].reshape(width, lane))
                nhi[j * width:(j + 1) * width, h * lane:(h + 1) * lane] = high
                nlo[j * width:(j + 1) * width, h * lane:(h + 1) * lane] = low

        @pl.loop(0, CAP // 2)
        def _(m):
            one, two = ids[s, 2 * m], ids[s, 2 * m + 1]
            high = jnp.concatenate([ahi[one], ahi[two]], axis=0)
            low = jnp.concatenate([alo[one], alo[two]], axis=0)
            total = jnp.dot(high, nhi[...], preferred_element_type=F32)
            total += jnp.dot(high, nlo[...], preferred_element_type=F32)
            total += jnp.dot(low, nhi[...], preferred_element_type=F32)
            rows = ahi.shape[1]
            ybuf[s, :, 2 * m] = total[:rows].reshape(NZ, 2, sub, width)
            ybuf[s, :, 2 * m + 1] = total[rows:].reshape(NZ, 2, sub, width)
        b = lax.rem(z - way + NZ, NZ)
        send(ybuf.at[s, b], rbuf.at[s, 0], ring_s.at[s, 0], ring_r.at[s, 0], onward)

    def ring(s, t):
        wait_for(rbuf.at[s, t], ring_r.at[s, t])
        b = lax.rem(z - way * (t + 2) + 2 * NZ, NZ)
        ybuf[s, b] = ybuf[s, b] + rbuf[s, t]

        @pl.when(t < NZ - 2)
        def _():
            send(ybuf.at[s, b], rbuf.at[s, t + 1], ring_s.at[s, t + 1], ring_r.at[s, t + 1], onward)

        @pl.when(t == NZ - 2)
        def _():
            send(ybuf.at[s, z, :, 1 - yh], pbuf.at[s], p_s.at[s], p_r.at[s], across)

    def finish(s):
        wait_for(pbuf.at[s], p_r.at[s])
        yfin[s] = ybuf[s, z, :, yh] + pbuf[s]
        for k in range(slots):
            off[s, k] = yfin[s, pos[s, k]] * (-mask[s, k].astype(F32))
        part = -lax.dot_general(
            nflat[s], off[s].reshape(slots * sub, width), (((0,), (0,)), ((), ())),
            precision=HIGHEST, preferred_element_type=F32,
        )
        for h in range(2):
            dbuf[s, :, h * 4:(h + 1) * 4] = part[:, h * lane:(h + 1) * lane].reshape(NR, 4, sub, lane)
        drow[s, r] = dbuf[s, r]

        @pl.loop(1, NR)
        def _(i):
            p = row_peer(i)
            send(dbuf.at[s, p], drow.at[s, r], d_s.at[s, 0], d_r.at[s, 0], {"row": p, "col": c})

    def diag_z(s):
        wait_for(drow.at[s, pl.ds(0, NR - 1)], d_r.at[s, 0])
        ebuf[s] = jnp.sum(drow[s], axis=0)
        ez[s, z] = ebuf[s, z]

        @pl.loop(1, NZ)
        def _(i):
            t = z_peer(i)
            send(ebuf.at[s, t], ez.at[s, z], d_s.at[s, 1], d_r.at[s, 1], dev(r, t, q))

    def diag_q(s):
        wait_for(ez.at[s, pl.ds(0, NZ - 1)], d_r.at[s, 1])
        fq[s, q] = jnp.sum(ez[s], axis=0)
        for i in range(1, 4):
            send(fq.at[s, q], fq.at[s, q], d_s.at[s, 2], d_r.at[s, 2], dev(r, z, lax.rem(q + i, 4)))

    def spread_z(s):
        wait_for(fq.at[s, pl.ds(0, 3)], d_r.at[s, 2])
        gr[s, r, z] = (fq[s, 0] + fq[s, 1]) + (fq[s, 2] + fq[s, 3])

        @pl.loop(1, NZ)
        def _(i):
            send(gr.at[s, r, z], gr.at[s, r, z], d_s.at[s, 3], d_r.at[s, 3], dev(r, z_peer(i), q))

    def spread_row(s):
        wait_for(gr.at[s, r, pl.ds(0, NZ - 1)], d_r.at[s, 3])

        @pl.loop(1, NR)
        def _(i):
            send(gr.at[s, r], gr.at[s, r], d_s.at[s, 4], d_r.at[s, 4], {"row": row_peer(i), "col": c})

    def gather_diag(s):
        wait_for(gr.at[s, pl.ds(0, NR - 1)], d_r.at[s, 4])
        for h in range(2):
            here = slice(h * lane, (h + 1) * lane)
            diag[s, :, here] = lead[s, :, here] + gr[s, :, h * 4:(h + 1) * 4].reshape(width, lane)

    last = LAG + NZ
    after = (gather_diag, spread_row, spread_z, diag_q, diag_z, finish)
    before = (multiply, share, relay_three, relay_two, relay_one)

    @pl.loop(0, nodes + last + len(after) - 1)
    def _(n):
        def at(lag, work):
            s = n - lag

            @pl.when((s >= 0) & (s < nodes))
            def _():
                work(s)

        for i, work in enumerate(after):
            at(last + len(after) - 1 - i, work)

        @pl.loop(0, NZ - 1)
        def _(i):
            t = NZ - 2 - i
            s = n - (LAG + 1) - t

            @pl.when((s >= 0) & (s < nodes))
            def _():
                ring(s, t)

        for i, work in enumerate(before):
            at(LAG - i, work)

    wait_for(af.at[core], a_sem.at[1])
    for g in range(groups):
        wait_for(abuf.at[g, pl.ds(0, NR - 1)], s1_s.at[g])
        wait_for(nbuf.at[pl.ds(0, group), r, pl.ds(0, 2 * NZ - 1), core], s2_s.at[g])

    @pl.loop(0, nodes)
    def _(s):
        wait_for(block(s, r), c1_s.at[s])
        for w in range(2):
            wait_for(nbuf.at[s, pl.ds(0, 2), :, core], c2_s.at[s, w])
            wait_for(block(s, r), c3_s.at[s, w])
        wait_for(nbuf.at[s, :, :, core], sh_s.at[s])

        @pl.loop(0, NZ - 1)
        def _(t):
            wait_for(rbuf.at[s, t], ring_s.at[s, t])

        wait_for(pbuf.at[s], p_s.at[s])
        wait_for(drow.at[s, pl.ds(0, NR - 1)], d_s.at[s, 0])
        wait_for(ez.at[s, pl.ds(0, NZ - 1)], d_s.at[s, 1])
        wait_for(fq.at[s, pl.ds(0, 3)], d_s.at[s, 2])
        wait_for(gr.at[s, r, pl.ds(0, NZ - 1)], d_s.at[s, 3])
        wait_for(gr.at[s, pl.ds(0, NR - 1)], d_s.at[s, 4])


def body(ancestor_inverse, panel, diag_inverse, structure, block_slot):
    nodes, slots, sub, width = panel.shape
    total = slots * NR
    group = 2 if nodes % 2 == 0 else 1
    groups = nodes // group
    lane = width // 2
    r = lax.axis_index("row")
    slot_range = jnp.arange(total, dtype=jnp.int32)
    lookup = (structure[:, :, None] == slot_range[None, None, :]).astype(jnp.int32)
    slot_ids = jnp.sum(lookup * block_slot[None, None, :], axis=2)
    local = jnp.arange(slots, dtype=jnp.int32)
    near = slot_ids[:, :, None] == (local + r * slots)[None, None, :]
    mask = jnp.sum(near.astype(jnp.int32), axis=1)
    pos = jnp.sum(mask[:, None, :] * (local[None, :] < local[:, None]).astype(jnp.int32)[None], axis=2) * mask
    place = jnp.arange(CAP, dtype=jnp.int32)
    ids = jnp.sum((pos[:, None, :] == place[None, :, None]) * mask[:, None, :] * local[None, None, :], axis=2)

    blocks = ancestor_inverse.reshape(slots, 2 * NZ, 2, sub, 2 * width)
    rows, depth = slots * 0 + width // 2, 4 * width
    vmem = pl.BlockSpec(memory_space=pltpu.VMEM)
    smem = pl.BlockSpec(memory_space=pltpu.SMEM)
    dma = pltpu.SemaphoreType.DMA
    return pl.pallas_call(
        functools.partial(kernel, group),
        out_shape=(
            jax.ShapeDtypeStruct((nodes, slots, sub, width), F32),
            jax.ShapeDtypeStruct((nodes, width, width), F32),
        ),
        in_specs=[smem, smem, smem, pl.BlockSpec(memory_space=pl.ANY), vmem, vmem],
        out_specs=(vmem, vmem),
        scratch_shapes=[
            pltpu.VMEM((2, slots, 2 * NZ, sub, 2 * width), F32),
            pltpu.VMEM((slots, rows, depth), BF16),
            pltpu.VMEM((slots, rows, depth), BF16),
            pltpu.VMEM((nodes, 2, NR, sub, lane), F32),
            pltpu.VMEM((nodes, slots * sub, width), F32),
            pltpu.VMEM((groups, NR, group, 2, sub, lane), F32),
            pltpu.VMEM((nodes, NR, 2 * NZ, 2, sub, lane), F32),
            pltpu.VMEM((depth, width), BF16),
            pltpu.VMEM((depth, width), BF16),
            pltpu.VMEM((nodes, NZ, CAP, 2, sub, width), F32),
            pltpu.VMEM((nodes, NZ - 1, CAP, 2, sub, width), F32),
            pltpu.VMEM((nodes, CAP, sub, width), F32),
            pltpu.VMEM((nodes, CAP, sub, width), F32),
            pltpu.VMEM((nodes, NR, NZ, sub, lane), F32),
            pltpu.VMEM((nodes, NR, NZ, sub, lane), F32),
            pltpu.VMEM((nodes, NZ, sub, lane), F32),
            pltpu.VMEM((nodes, NZ, sub, lane), F32),
            pltpu.VMEM((nodes, 4, sub, lane), F32),
            pltpu.VMEM((nodes, NR, NZ, sub, lane), F32),
            pltpu.VMEM((nodes, width, width), F32),
            dma((3,)),
            dma((groups,)), dma((groups,)), dma((groups,)),
            dma((groups,)), dma((groups,)), dma((groups,)),
            dma((nodes,)), dma((nodes,)),
            dma((nodes, 2)), dma((nodes, 2)),
            dma((nodes, 2)), dma((nodes, 2)),
            dma((nodes,)), dma((nodes,)),
            dma((nodes, NZ - 1)), dma((nodes, NZ - 1)),
            dma((nodes,)), dma((nodes,)),
            dma((nodes, 5)), dma((nodes, 5)),
        ],
        compiler_params=pltpu.CompilerParams(
            collective_id=0, has_side_effects=True, vmem_limit_bytes=62 * 1024 * 1024
        ),
        name="invert_level",
    )(ids, pos, mask, blocks, panel, diag_inverse)


def solution(mesh):
    in_specs = (P("row", "col"), P(None, "row", "col", None), P(), P(), P())
    out_specs = (P(None, "row", "col", None), P())
    return jax.shard_map(body, mesh=mesh, in_specs=in_specs, out_specs=out_specs, check_vma=False)
```

time: 786 us -> 160 us (0.20)
  waiting for transfers between devices: 712 us -> 0 us
  Pallas kernels: 0 us -> 151 us
  matrix products: 36.6 us -> 0 us
  between operations: 13.8 us -> 0.69 us
  local copies, waits for them, and re-layouts: 16.3 us -> 4.52 us
    psum x2 -> x0, waiting for transfers between devices: 407 us -> none  [the longest x1 264 us: body(): diag_sum = lax.psum(diag_terms, ('row', 'col'))]
    reduce_scatter x1 -> x0, waiting for transfers between devices: 170 us -> none  [body(): lax.psum_scatter(partial_value, 'col', scatter_dimension=2, tiled=True)]
    pallas_call x0 -> x1, Pallas kernels: none -> 151 us  [body(): pl.pallas_call(functools.partial(kernel, group), out_shape=(jax.ShapeDtyp...]
    all_gather x1 -> x0, waiting for transfers between devices: 134 us -> none  [gather_rows(): return lax.all_gather(normalized, 'col', axis=2, tiled=True)]
    dot_general x4 -> x0, matrix products: 36.6 us -> none  [the longest x1 24.8 us: body(): jnp.einsum('rc,scw->srw', ancestor_inverse, column_rows, precision=highest)]
    transpose x1 -> x0, local copies, waits for them, and re-layouts: 12.6 us -> none  [body(): jnp.einsum('rc,scw->srw', ancestor_inverse, column_rows, precision=highest)]
  transfers between devices with their start and end apart: 4 -> 0, of which waited for: 4 -> 0; matrix products, arithmetic and copies ran while one was open for 0% -> 0% of each run, Pallas kernels for 0% -> 0%
where the time goes in v1:
time: 160 us; the launch traced here: 158 us
  Pallas kernels  151 us (94%)
  local copies, waits for them, and re-layouts  4.52 us (3%)
  other arithmetic  2.15 us (1%)
    pallas_call x1, Pallas kernels, body(): pl.pallas_call(functools.partial(kernel, group), out_shape=(jax.ShapeDtyp...  151 us
    unnamed x6, local copies, waits for them, and re-layouts  4.52 us

profile of v1, /device:TPU:1, one launch (start us, length us, event | category | flops | bytes accessed | tf_op | source)
XLA Modules:
  0.0 158.4 jit_solution(5834060879271351567)
XLA Ops:
  0.6 1.0 select_reduce_fusion
  1.6 0.2 convert_reduce_fusion.mask
  1.9 0.0 copy-start
  1.9 0.2 multiply_reduce_fusion.1
  2.1 0.0 copy-start.1
  2.1 0.8 multiply_reduce_fusion.ids
  2.8 0.0 copy-done
  2.8 0.0 copy-done.1
  2.9 151.0 %invert_level.1 = (f32[6,8,8,256]{3,2,1,0:T(8,128)}, f32[6,256,256]{2,1,0:T(8,128)}) custom-call(s32[6,6]{1,0:T(8,128)} %multiply_reduce_fusion.ids, s32[6,8]{1,0:T(8,128)} %copy-done.1, s32[6,8]{1,0:T(8,128)} %copy-done, f32[8,16,2,8,512]{4,3,2,1,0:T(8,128)} %bitcast.1, f32[6,8,8,256]{3,2,1,0:T(8,128)} %panel.1, f32[6,256,256]{2,1,0:T(8,128)} %dinv.1), custom_call_target="tpu_custom_call" | custom-call | tf_op jit(solution)/shard_map/invert_level/pallas_call | solution.py:350
  153.9 1.8 %copy.9 = f32[6,8,8,256]{3,2,1,0:T(8,128)} copy(f32[6,8,8,256]{3,2,1,0:T(8,128)} %get-tuple-element.4) | data formatting | bytes 786432
  155.6 2.7 %copy.10 = f32[6,256,256]{2,1,0:T(8,128)} copy(f32[6,256,256]{2,1,0:T(8,128)} %get-tuple-element.5) | data formatting | bytes 3145728
  (3 shorter events, 0.0 us)
Async XLA Ops:
  1.9 1.0 copy-start
  2.1 0.8 copy-start.1

commit v2 on v1

v2 whole, which is shorter than its diff:
```python
import functools

import jax
import jax.numpy as jnp
from jax import lax
from jax.experimental import pallas as pl
from jax.experimental.pallas import tpu as pltpu
from jax.sharding import PartitionSpec as P

F32 = jnp.float32
BF16 = jnp.bfloat16
MESH = pl.DeviceIdType.MESH
HIGHEST = lax.Precision.HIGHEST

NR = 8
NZ = 8
CAP = 6
LAG = 3


def halves(value):
    high = value.astype(BF16)
    return high, (value - high.astype(F32)).astype(BF16)


def wait_for(ref, sem):
    pltpu.make_async_copy(ref, ref, sem).wait()


def kernel(
    group,
    structure, place, a_ref, panel_ref, dinv_ref, off, diag,
    ids, pos, mask, panel, dinv,
    af, ahi, alo, nsrc, nboth, abuf, nbuf, nhi, nlo, ybuf, rbuf, pbuf, yfin, fexp,
    dbuf, drow, ebuf, ez, gr, lead,
    in_sem, a_sem, s1_s, s1_r, s1_l, s2_s, s2_r, s2_l,
    c1_s, c1_r, c2_s, c2_r, c3_s, c3_r, sh_s, sh_r, n_s, n_r,
    ring_s, ring_r, p_s, p_r, d_s, d_r,
):
    nodes, slots, sub, width = panel.shape
    lane = width // 2
    flat = slots * sub
    groups = nodes // group
    r = lax.axis_index("row")
    c = lax.axis_index("col")
    z = c // 4
    yh = lax.rem(c // 2, 2)
    core = lax.rem(c, 2)
    zy = c // 2
    rc = r * 2 + core
    x = r // 2
    yl = lax.rem(r, 2)

    def send(src, dst, ssem, rsem, where):
        pltpu.make_async_remote_copy(
            src_ref=src, dst_ref=dst, send_sem=ssem, recv_sem=rsem,
            device_id=where, device_id_type=MESH,
        ).start()

    def at_rc(t):
        return {"row": t // 2, "col": zy * 2 + lax.rem(t, 2)}

    def at_zy(t):
        return {"row": r, "col": t * 2 + core}

    def rc_peer(i):
        return lax.rem(rc + i, 2 * NR)

    def zy_peer(i):
        return lax.rem(zy + i, 2 * NZ)

    mate = {"row": r, "col": zy * 2 + 1 - core}
    across = at_zy(z * 2 + 1 - yh)

    load_panel = pltpu.make_async_copy(panel_ref, panel, in_sem.at[0])
    load_dinv = pltpu.make_async_copy(dinv_ref, dinv, in_sem.at[1])
    own_a = pltpu.make_async_copy(a_ref.at[:, :, core], af.at[core], a_sem.at[0])
    load_panel.start()
    load_dinv.start()
    own_a.start()

    barrier = pltpu.get_barrier_semaphore()

    @pl.loop(1, 2 * NR)
    def _(i):
        pl.semaphore_signal(barrier, inc=1, device_id=at_rc(rc_peer(i)), device_id_type=MESH)
        pl.semaphore_signal(barrier, inc=1, device_id=at_zy(zy_peer(i)), device_id_type=MESH)

    @pl.loop(0, nodes)
    def _(s):
        def count(k, seen):
            slot = place[structure[s, k]] - r * slots
            return tuple(n + (slot == i).astype(jnp.int32) for i, n in enumerate(seen))

        seen = lax.fori_loop(0, structure.shape[1], count, (jnp.int32(0),) * slots)
        before = jnp.int32(0)
        spots = []
        for i in range(slots):
            mask[s, i] = seen[i]
            pos[s, i] = before * seen[i]
            spots.append(before)
            before = before + seen[i]
        for k in range(CAP):
            found = jnp.int32(0)
            for i in range(slots):
                found = found + i * seen[i] * (spots[i] == k).astype(jnp.int32)
            ids[s, k] = found

    load_panel.wait()
    load_dinv.wait()

    @pl.loop(0, nodes)
    def _(s):
        value = jnp.dot(
            panel[s].reshape(flat, width), dinv[s],
            precision=HIGHEST, preferred_element_type=F32,
        )
        for k in range(slots):
            part = value[k * sub:(k + 1) * sub] * mask[s, k].astype(F32)
            nboth[s, 0, k * sub:(k + 1) * sub, :] = part
            for h in range(2):
                nsrc[s, k // 4, (k % 4) * 2 + h] = part[:, h * lane:(h + 1) * lane]

    pl.semaphore_wait(barrier, 2 * (2 * NR - 1))

    for g in range(groups):
        span = pl.ds(g * group, group)
        pltpu.make_async_copy(nsrc.at[span, :, r], abuf.at[g, r], s1_l.at[g]).start()

        @pl.loop(1, NR)
        def _(i):
            p = lax.rem(r + i, NR)
            send(nsrc.at[span, :, p], abuf.at[g, r], s1_s.at[g], s1_r.at[g], {"row": p, "col": c})

    send(a_ref.at[:, :, 1 - core], af.at[core], a_sem.at[1], a_sem.at[2], mate)

    for g in range(groups):
        span = pl.ds(g * group, group)
        wait_for(abuf.at[g, r], s1_l.at[g])
        wait_for(abuf.at[g, pl.ds(0, NR - 1)], s1_r.at[g])
        pltpu.make_async_copy(abuf.at[g, z, :, yh], nbuf.at[span, r, zy, core], s2_l.at[g]).start()

        @pl.loop(1, 2 * NZ)
        def _(i):
            t = zy_peer(i)
            send(
                abuf.at[g, t // 2, :, lax.rem(t, 2)], nbuf.at[span, r, zy, core],
                s2_s.at[g], s2_r.at[g], at_zy(t),
            )

    right = {"row": lax.rem(x + 1, 4) * 2 + yl, "col": c}
    left = {"row": lax.rem(x + 3, 4) * 2 + yl, "col": c}
    other = x * 2 + 1 - yl
    twin = {"row": other, "col": c}
    xl, xr, xo = lax.rem(x + 3, 4), lax.rem(x + 1, 4), lax.rem(x + 2, 4)
    way = 1 - 2 * core
    onward = at_zy(lax.rem(z + way + NZ, NZ) * 2 + yh)

    def block(s, p):
        return nbuf.at[s, p, :, core]

    def two(s, p):
        return nbuf.at[s, pl.ds(p, 2), :, core]

    def share(s, part):
        send(part, part, sh_s.at[s], sh_r.at[s], mate)

    def relay_one(s):
        @pl.when(lax.rem(s, group) == 0)
        def _():
            g = s // group
            wait_for(nbuf.at[pl.ds(0, group), r, zy, core], s2_l.at[g])
            wait_for(nbuf.at[pl.ds(0, group), r, pl.ds(0, 2 * NZ - 1), core], s2_r.at[g])
        mine = block(s, r)
        send(mine, mine, c1_s.at[s], c1_r.at[s], twin)
        send(mine, mine, c2_s.at[s, 0], c2_r.at[s, 0], right)
        send(mine, mine, c2_s.at[s, 1], c2_r.at[s, 1], left)
        share(s, mine)

    def relay_two(s):
        wait_for(block(s, r), c1_r.at[s])
        theirs = block(s, other)
        send(theirs, theirs, c2_s.at[s, 0], c2_r.at[s, 0], right)
        send(theirs, theirs, c2_s.at[s, 1], c2_r.at[s, 1], left)
        share(s, theirs)

    def relay_three(s):
        wait_for(two(s, 0), c2_r.at[s, 0])
        send(block(s, 2 * xl), block(s, 2 * xl), c3_s.at[s, 0], c3_r.at[s, 0], right)
        share(s, two(s, 2 * xl))
        wait_for(two(s, 0), c2_r.at[s, 1])
        send(block(s, 2 * xr + 1), block(s, 2 * xr + 1), c3_s.at[s, 1], c3_r.at[s, 1], left)
        share(s, two(s, 2 * xr))

    def relay_four(s):
        wait_for(block(s, r), c3_r.at[s, 0])
        wait_for(block(s, r), c3_r.at[s, 1])
        share(s, two(s, 2 * xo))

    def multiply(s):
        wait_for(nbuf.at[s, :, :, 1 - core], sh_r.at[s])
        for j in range(4):
            for h in range(2):
                high, low = halves(nbuf[s, 2 * j + h].reshape(width, lane))
                nhi[j * width:(j + 1) * width, h * lane:(h + 1) * lane] = high
                nlo[j * width:(j + 1) * width, h * lane:(h + 1) * lane] = low

        @pl.loop(0, CAP // 2)
        def _(m):
            one, two = ids[s, 2 * m], ids[s, 2 * m + 1]
            high = jnp.concatenate([ahi[one], ahi[two]], axis=0)
            low = jnp.concatenate([alo[one], alo[two]], axis=0)
            total = jnp.dot(high, nhi[...], preferred_element_type=F32)
            total += jnp.dot(high, nlo[...], preferred_element_type=F32)
            total += jnp.dot(low, nhi[...], preferred_element_type=F32)
            rows = ahi.shape[1]
            ybuf[s, :, 2 * m] = total[:rows].reshape(NZ, 2, sub, width)
            ybuf[s, :, 2 * m + 1] = total[rows:].reshape(NZ, 2, sub, width)
        b = lax.rem(z - way + NZ, NZ)
        send(ybuf.at[s, b], rbuf.at[s, 0], ring_s.at[s, 0], ring_r.at[s, 0], onward)
        send(nboth.at[s, 0], nboth.at[s, 1], n_s.at[s], n_r.at[s], across)

    def ring(s, t):
        wait_for(rbuf.at[s, t], ring_r.at[s, t])
        b = lax.rem(z - way * (t + 2) + 2 * NZ, NZ)
        ybuf[s, b] = ybuf[s, b] + rbuf[s, t]

        @pl.when(t < NZ - 2)
        def _():
            send(ybuf.at[s, b], rbuf.at[s, t + 1], ring_s.at[s, t + 1], ring_r.at[s, t + 1], onward)

        @pl.when(t == NZ - 2)
        def _():
            send(ybuf.at[s, z, :, 1 - yh], pbuf.at[s], p_s.at[s], p_r.at[s], across)
            wait_for(nboth.at[s, 1], n_r.at[s])
            for k in range(slots):
                scale = mask[s, k].astype(F32)
                fexp[k * sub:(k + 1) * sub, :] = ybuf[s, z, pos[s, k], yh] * scale
                fexp[flat + k * sub:flat + (k + 1) * sub, :] = ybuf[s, z, pos[s, k], 1 - yh] * scale
            part = lax.dot_general(
                nboth[s].reshape(2 * flat, width), fexp[...], (((0,), (0,)), ((), ())),
                precision=HIGHEST, preferred_element_type=F32,
            )
            for h in range(2):
                dbuf[s, :, h] = part[:, h * lane:(h + 1) * lane].reshape(NR, 4, sub, lane)
            drow[s, rc] = dbuf[s, r, core]

            @pl.loop(1, 2 * NR)
            def _(i):
                p = rc_peer(i)
                send(dbuf.at[s, p // 2, lax.rem(p, 2)], drow.at[s, rc], d_s.at[s, 0], d_r.at[s, 0], at_rc(p))

    def finish(s):
        wait_for(pbuf.at[s], p_r.at[s])
        yfin[...] = ybuf[s, z, :, yh] + pbuf[s]
        for k in range(slots):
            off[s, k] = yfin[pos[s, k]] * (-mask[s, k].astype(F32))

    def diag_z(s):
        wait_for(drow.at[s, pl.ds(0, 2 * NR - 1)], d_r.at[s, 0])
        ebuf[s] = jnp.sum(drow[s], axis=0)
        ez[s, zy] = ebuf[s, lax.rem(z, 4)]

        @pl.loop(1, 2 * NZ)
        def _(i):
            t = zy_peer(i)
            send(ebuf.at[s, lax.rem(t // 2, 4)], ez.at[s, zy], d_s.at[s, 1], d_r.at[s, 1], at_zy(t))

    def spread_z(s):
        wait_for(ez.at[s, pl.ds(0, 2 * NZ - 1)], d_r.at[s, 1])
        u = lax.rem(z, 4)
        gr[s, rc, u] = jnp.sum(ez[s], axis=0)
        for i in range(1, 4):
            t = (z // 4) * 4 + lax.rem(z + i, 4)
            send(gr.at[s, rc, u], gr.at[s, rc, u], d_s.at[s, 2], d_r.at[s, 2], at_zy(t * 2 + yh))

    def spread_row(s):
        wait_for(gr.at[s, rc, pl.ds(0, 3)], d_r.at[s, 2])

        @pl.loop(1, 2 * NR)
        def _(i):
            send(gr.at[s, rc], gr.at[s, rc], d_s.at[s, 3], d_r.at[s, 3], at_rc(rc_peer(i)))

    def gather_diag(s):
        wait_for(gr.at[s, pl.ds(0, 2 * NR - 1)], d_r.at[s, 3])
        whole = gr[s].reshape(NR, 2, 4, sub, lane)
        for h in range(2):
            here = slice(h * lane, (h + 1) * lane)
            diag[s, :, here] = lead[s, :, here] + whole[:, h].reshape(width, lane)

    def leading(s):
        lead[s] = lax.dot_general(
            dinv[s], dinv[s], (((0,), (0,)), ((), ())),
            precision=HIGHEST, preferred_element_type=F32,
        )

    last = LAG + NZ - 1
    stages = (
        (last + 4, gather_diag), (last + 3, spread_row), (last + 2, spread_z), (last + 1, diag_z),
        None,
        (3, relay_four), (2, relay_three), (1, relay_two), (0, relay_one),
        (LAG, multiply), (last + 1, finish), (LAG + 1, leading),
    )

    @pl.loop(0, nodes + last + 4)
    def _(n):
        for entry in stages:
            if entry is None:
                @pl.loop(0, NZ - 1)
                def _(i):
                    t = NZ - 2 - i
                    s = n - (LAG + 1) - t

                    @pl.when((s >= 0) & (s < nodes))
                    def _():
                        ring(s, t)
            else:
                lag, work = entry
                s = n - lag

                @pl.when((s >= 0) & (s < nodes))
                def _():
                    work(s)

        @pl.when(n == LAG - 1)
        def _():
            wait_for(af.at[core], a_sem.at[0])
            wait_for(af.at[1 - core], a_sem.at[2])

            @pl.loop(0, slots)
            def _(k):
                for h in range(2):
                    rows, cols = ahi.shape[1], ahi.shape[2] // 2
                    high, low = halves(af[h, k].reshape(rows, cols))
                    ahi[k, :, h * cols:(h + 1) * cols] = high
                    alo[k, :, h * cols:(h + 1) * cols] = low

    wait_for(af.at[core], a_sem.at[1])
    for g in range(groups):
        wait_for(abuf.at[g, pl.ds(0, NR - 1)], s1_s.at[g])
        wait_for(nbuf.at[pl.ds(0, group), r, pl.ds(0, 2 * NZ - 1), core], s2_s.at[g])

    @pl.loop(0, nodes)
    def _(s):
        wait_for(block(s, r), c1_s.at[s])
        for w in range(2):
            wait_for(two(s, 0), c2_s.at[s, w])
            wait_for(block(s, r), c3_s.at[s, w])
        wait_for(nbuf.at[s, :, :, core], sh_s.at[s])
        wait_for(nboth.at[s, 0], n_s.at[s])

        @pl.loop(0, NZ - 1)
        def _(t):
            wait_for(rbuf.at[s, t], ring_s.at[s, t])

        wait_for(pbuf.at[s], p_s.at[s])
        wait_for(drow.at[s, pl.ds(0, 2 * NR - 1)], d_s.at[s, 0])
        wait_for(ez.at[s, pl.ds(0, 2 * NZ - 1)], d_s.at[s, 1])
        wait_for(gr.at[s, rc, pl.ds(0, 3)], d_s.at[s, 2])
        wait_for(gr.at[s, pl.ds(0, 2 * NR - 1)], d_s.at[s, 3])


def body(ancestor_inverse, panel, diag_inverse, structure, block_slot):
    nodes, slots, sub, width = panel.shape
    group = 2 if nodes % 2 == 0 else 1
    groups = nodes // group
    lane = width // 2
    flat = slots * sub
    blocks = ancestor_inverse.reshape(slots, 2 * NZ, 2, sub, 2 * width)
    rows, depth = width // 2, 4 * width
    vmem = pl.BlockSpec(memory_space=pltpu.VMEM)
    smem = pl.BlockSpec(memory_space=pltpu.SMEM)
    hbm = pl.BlockSpec(memory_space=pl.ANY)
    dma = pltpu.SemaphoreType.DMA
    return pl.pallas_call(
        functools.partial(kernel, group),
        out_shape=(
            jax.ShapeDtypeStruct((nodes, slots, sub, width), F32),
            jax.ShapeDtypeStruct((nodes, width, width), F32),
        ),
        in_specs=[smem, smem, hbm, hbm, hbm],
        out_specs=(vmem, vmem),
        scratch_shapes=[
            pltpu.SMEM((nodes, CAP), jnp.int32),
            pltpu.SMEM((nodes, slots), jnp.int32),
            pltpu.SMEM((nodes, slots), jnp.int32),
            pltpu.VMEM((nodes, slots, sub, width), F32),
            pltpu.VMEM((nodes, width, width), F32),
            pltpu.VMEM((2, slots, 2 * NZ, sub, 2 * width), F32),
            pltpu.VMEM((slots, rows, depth), BF16),
            pltpu.VMEM((slots, rows, depth), BF16),
            pltpu.VMEM((nodes, 2, NR, sub, lane), F32),
            pltpu.VMEM((nodes, 2, flat, width), F32),
            pltpu.VMEM((groups, NR, group, 2, sub, lane), F32),
            pltpu.VMEM((nodes, NR, 2 * NZ, 2, sub, lane), F32),
            pltpu.VMEM((depth, width), BF16),
            pltpu.VMEM((depth, width), BF16),
            pltpu.VMEM((nodes, NZ, CAP, 2, sub, width), F32),
            pltpu.VMEM((nodes, NZ - 1, CAP, 2, sub, width), F32),
            pltpu.VMEM((nodes, CAP, sub, width), F32),
            pltpu.VMEM((CAP, sub, width), F32),
            pltpu.VMEM((2 * flat, width), F32),
            pltpu.VMEM((nodes, NR, 2, 4, sub, lane), F32),
            pltpu.VMEM((nodes, 2 * NR, 4, sub, lane), F32),
            pltpu.VMEM((nodes, 4, sub, lane), F32),
            pltpu.VMEM((nodes, 2 * NZ, sub, lane), F32),
            pltpu.VMEM((nodes, 2 * NR, 4, sub, lane), F32),
            pltpu.VMEM((nodes, width, width), F32),
            dma((2,)), dma((3,)),
            dma((groups,)), dma((groups,)), dma((groups,)),
            dma((groups,)), dma((groups,)), dma((groups,)),
            dma((nodes,)), dma((nodes,)),
            dma((nodes, 2)), dma((nodes, 2)),
            dma((nodes, 2)), dma((nodes, 2)),
            dma((nodes,)), dma((nodes,)),
            dma((nodes,)), dma((nodes,)),
            dma((nodes, NZ - 1)), dma((nodes, NZ - 1)),
            dma((nodes,)), dma((nodes,)),
            dma((nodes, 4)), dma((nodes, 4)),
        ],
        compiler_params=pltpu.CompilerParams(
            collective_id=0, has_side_effects=True, vmem_limit_bytes=62 * 1024 * 1024
        ),
        name="invert_level",
    )(structure, block_slot, blocks, panel, diag_inverse)


def solution(mesh):
    in_specs = (P("row", "col"), P(None, "row", "col", None), P(), P(), P())
    out_specs = (P(None, "row", "col", None), P())
    return jax.shard_map(body, mesh=mesh, in_specs=in_specs, out_specs=out_specs, check_vma=False)
```

time: 160 us -> 154 us (0.963)
  Pallas kernels: 151 us -> 148 us
  other arithmetic: 2.15 us -> 0 us
    pallas_call x1, Pallas kernels: 151 us -> 148 us  [body(): pl.pallas_call(functools.partial(kernel, group), out_shape=(jax.ShapeDtyp...]
    reduce_sum x4 -> x0, other arithmetic: 2.14 us -> none  [the longest x1 0.96 us: body(): slot_ids = jnp.sum(lookup * block_slot[None, None, :], axis=2)]
    unnamed x6 -> x2, local copies, waits for them, and re-layouts: 4.52 us -> 4.51 us
where the time goes in v2:
time: 154 us; the launch traced here: 153 us
  Pallas kernels  148 us (96%)
  local copies, waits for them, and re-layouts  4.51 us (3%)
    pallas_call x1, Pallas kernels, body(): pl.pallas_call(functools.partial(kernel, group), out_shape=(jax.ShapeDtyp...  148 us
    unnamed x2, local copies, waits for them, and re-layouts  4.51 us

profile of v2, /device:TPU:1, one launch (start us, length us, event | category | flops | bytes accessed | tf_op | source)
XLA Modules:
  0.0 153.4 jit_solution(4684100130042994566)
XLA Ops:
  0.6 148.2 %invert_level.1 = (f32[6,8,8,256]{3,2,1,0:T(8,128)}, f32[6,256,256]{2,1,0:T(8,128)}) custom-call(s32[6,32]{1,0:T(8,128)} %structure.1, s32[64]{0:T(128)} %place.1, f32[8,16,2,8,512]{4,3,2,1,0:T(8,128)} %bitcast.1, f32[6,8,8,256]{3,2,1,0:T(8,128)} %panel_ref.1, f32[6,256,256]{2,1,0:T(8,128)} %dinv_ref.1), custom_call_target="tpu_custom_call" | custom-call | tf_op jit(solution)/shard_map/invert_level/pallas_call | solution.py:375
  148.9 1.8 %copy.9 = f32[6,8,8,256]{3,2,1,0:T(8,128)} copy(f32[6,8,8,256]{3,2,1,0:T(8,128)} %get-tuple-element.4) | data formatting | bytes 786432
  150.6 2.7 %copy.10 = f32[6,256,256]{2,1,0:T(8,128)} copy(f32[6,256,256]{2,1,0:T(8,128)} %get-tuple-element.5) | data formatting | bytes 3145728

commit v3 on v2

--- a/solution.py
+++ b/solution.py
@@ -30,7 +30,7 @@
 def kernel(
     group,
     structure, place, a_ref, panel_ref, dinv_ref, off, diag,
-    ids, pos, mask, panel, dinv,
+    bits, ids, pos, mask, panel, dinv,
     af, ahi, alo, nsrc, nboth, abuf, nbuf, nhi, nlo, ybuf, rbuf, pbuf, yfin, fexp,
     dbuf, drow, ebuf, ez, gr, lead,
     in_sem, a_sem, s1_s, s1_r, s1_l, s2_s, s2_r, s2_l,
@@ -86,13 +86,17 @@
         pl.semaphore_signal(barrier, inc=1, device_id=at_rc(rc_peer(i)), device_id_type=MESH)
         pl.semaphore_signal(barrier, inc=1, device_id=at_zy(zy_peer(i)), device_id_type=MESH)
 
+    @pl.loop(0, place.shape[0])
+    def _(b):
+        slot = place[b] - r * slots
+        bits[b] = sum((slot == i).astype(jnp.int32) * (1 << i) for i in range(slots))
+
     @pl.loop(0, nodes)
     def _(s):
-        def count(k, seen):
-            slot = place[structure[s, k]] - r * slots
-            return tuple(n + (slot == i).astype(jnp.int32) for i, n in enumerate(seen))
-
-        seen = lax.fori_loop(0, structure.shape[1], count, (jnp.int32(0),) * slots)
+        used = bits[structure[s, 0]]
+        for k in range(1, structure.shape[1]):
+            used = used + bits[structure[s, k]]
+        seen = [lax.shift_right_logical(used, jnp.int32(i)) & 1 for i in range(slots)]
         before = jnp.int32(0)
         spots = []
         for i in range(slots):
@@ -123,7 +127,7 @@
 
     pl.semaphore_wait(barrier, 2 * (2 * NR - 1))
 
-    for g in range(groups):
+    def exchange_row(g):
         span = pl.ds(g * group, group)
         pltpu.make_async_copy(nsrc.at[span, :, r], abuf.at[g, r], s1_l.at[g]).start()
 
@@ -132,9 +136,7 @@
             p = lax.rem(r + i, NR)
             send(nsrc.at[span, :, p], abuf.at[g, r], s1_s.at[g], s1_r.at[g], {"row": p, "col": c})
 
-    send(a_ref.at[:, :, 1 - core], af.at[core], a_sem.at[1], a_sem.at[2], mate)
-
-    for g in range(groups):
+    def exchange_col(g):
         span = pl.ds(g * group, group)
         wait_for(abuf.at[g, r], s1_l.at[g])
         wait_for(abuf.at[g, pl.ds(0, NR - 1)], s1_r.at[g])
@@ -148,6 +150,17 @@
                 s2_s.at[g], s2_r.at[g], at_zy(t),
             )
 
+    exchange_row(0)
+    exchange_row(1)
+    send(a_ref.at[:, :, 1 - core], af.at[core], a_sem.at[1], a_sem.at[2], mate)
+    exchange_col(0)
+
+    @pl.loop(2, groups)
+    def _(g):
+        exchange_row(g)
+
+    exchange_col(1)
+
     right = {"row": lax.rem(x + 1, 4) * 2 + yl, "col": c}
     left = {"row": lax.rem(x + 3, 4) * 2 + yl, "col": c}
     other = x * 2 + 1 - yl
@@ -166,11 +179,13 @@
         send(part, part, sh_s.at[s], sh_r.at[s], mate)
 
     def relay_one(s):
-        @pl.when(lax.rem(s, group) == 0)
+        wait_for(nbuf.at[pl.ds(0, group), r, zy, core], s2_l.at[s])
+        wait_for(nbuf.at[pl.ds(0, group), r, pl.ds(0, 2 * NZ - 1), core], s2_r.at[s])
+
+        @pl.when(s + 2 < groups)
         def _():
-            g = s // group
-            wait_for(nbuf.at[pl.ds(0, group), r, zy, core], s2_l.at[g])
-            wait_for(nbuf.at[pl.ds(0, group), r, pl.ds(0, 2 * NZ - 1), core], s2_r.at[g])
+            exchange_col(s + 2)
+
         mine = block(s, r)
         send(mine, mine, c1_s.at[s], c1_r.at[s], twin)
         send(mine, mine, c2_s.at[s, 0], c2_r.at[s, 0], right)
@@ -296,13 +311,13 @@
 
     last = LAG + NZ - 1
     stages = (
-        (last + 4, gather_diag), (last + 3, spread_row), (last + 2, spread_z), (last + 1, diag_z),
         None,
-        (3, relay_four), (2, relay_three), (1, relay_two), (0, relay_one),
-        (LAG, multiply), (last + 1, finish), (LAG + 1, leading),
+        (3, relay_four), (LAG, multiply), (2, relay_three), (1, relay_two), (0, relay_one),
+        (last + 8, gather_diag), (last + 6, spread_row), (last + 4, spread_z), (last + 2, diag_z),
+        (last + 3, finish), (LAG + 1, leading),
     )
 
-    @pl.loop(0, nodes + last + 4)
+    @pl.loop(0, nodes + last + 8)
     def _(n):
         for entry in stages:
             if entry is None:
@@ -362,7 +377,7 @@
 
 def body(ancestor_inverse, panel, diag_inverse, structure, block_slot):
     nodes, slots, sub, width = panel.shape
-    group = 2 if nodes % 2 == 0 else 1
+    group = 1
     groups = nodes // group
     lane = width // 2
     flat = slots * sub
@@ -381,6 +396,7 @@
         in_specs=[smem, smem, hbm, hbm, hbm],
         out_specs=(vmem, vmem),
         scratch_shapes=[
+            pltpu.SMEM(block_slot.shape, jnp.int32),
             pltpu.SMEM((nodes, CAP), jnp.int32),
             pltpu.SMEM((nodes, slots), jnp.int32),
             pltpu.SMEM((nodes, slots), jnp.int32),

time: 154 us -> 140 us (0.909)
  Pallas kernels: 148 us -> 135 us
    pallas_call x1, Pallas kernels: 148 us -> 135 us  [body(): pl.pallas_call(functools.partial(kernel, group), out_shape=(jax.ShapeDtyp...]
where the time goes in v3:
time: 140 us
  Pallas kernels  135 us (96%)
  local copies, waits for them, and re-layouts  4.51 us (3%)
    pallas_call x1, Pallas kernels, body(): pl.pallas_call(functools.partial(kernel, group), out_shape=(jax.ShapeDtyp...  135 us
    unnamed x2, local copies, waits for them, and re-layouts  4.51 us

profile of v3, /device:TPU:1, one launch (start us, length us, event | category | flops | bytes accessed | tf_op | source)
XLA Modules:
  0.0 140.3 jit_solution(15818620959411467939)
XLA Ops:
  0.6 135.1 %invert_level.1 = (f32[6,8,8,256]{3,2,1,0:T(8,128)}, f32[6,256,256]{2,1,0:T(8,128)}) custom-call(s32[6,32]{1,0:T(8,128)} %structure.1, s32[64]{0:T(128)} %place.1, f32[8,16,2,8,512]{4,3,2,1,0:T(8,128)} %bitcast.1, f32[6,8,8,256]{3,2,1,0:T(8,128)} %panel_ref.1, f32[6,256,256]{2,1,0:T(8,128)} %dinv_ref.1), custom_call_target="tpu_custom_call" | custom-call | tf_op jit(solution)/shard_map/invert_level/pallas_call | solution.py:390
  135.8 1.8 %copy.9 = f32[6,8,8,256]{3,2,1,0:T(8,128)} copy(f32[6,8,8,256]{3,2,1,0:T(8,128)} %get-tuple-element.4) | data formatting | bytes 786432
  137.6 2.7 %copy.10 = f32[6,256,256]{2,1,0:T(8,128)} copy(f32[6,256,256]{2,1,0:T(8,128)} %get-tuple-element.5) | data formatting | bytes 3145728

commit v4 on v3

--- a/solution.py
+++ b/solution.py
@@ -29,11 +29,11 @@
 
 def kernel(
     group,
-    structure, place, a_ref, panel_ref, dinv_ref, off, diag,
-    bits, ids, pos, mask, panel, dinv,
+    structure, place, a_ref, panel_ref, dinv_ref, off_ref, diag_ref,
+    off, diag, bits, ids, pos, mask, panel, dinv,
     af, ahi, alo, nsrc, nboth, abuf, nbuf, nhi, nlo, ybuf, rbuf, pbuf, yfin, fexp,
-    dbuf, drow, ebuf, ez, gr, lead,
-    in_sem, a_sem, s1_s, s1_r, s1_l, s2_s, s2_r, s2_l,
+    dbuf, dmate, dsum, drow, ebuf, ez, gr, lead,
+    in_sem, o_sem, a_sem, s1_s, s1_r, s1_l, s2_s, s2_r, s2_l,
     c1_s, c1_r, c2_s, c2_r, c3_s, c3_r, sh_s, sh_r, n_s, n_r,
     ring_s, ring_r, p_s, p_r, d_s, d_r,
 ):
@@ -47,7 +47,6 @@
     yh = lax.rem(c // 2, 2)
     core = lax.rem(c, 2)
     zy = c // 2
-    rc = r * 2 + core
     x = r // 2
     yl = lax.rem(r, 2)
 
@@ -57,14 +56,14 @@
             device_id=where, device_id_type=MESH,
         ).start()
 
-    def at_rc(t):
-        return {"row": t // 2, "col": zy * 2 + lax.rem(t, 2)}
+    def at_row(t):
+        return {"row": t, "col": c}
 
     def at_zy(t):
         return {"row": r, "col": t * 2 + core}
 
-    def rc_peer(i):
-        return lax.rem(rc + i, 2 * NR)
+    def row_peer(i):
+        return lax.rem(r + i, NR)
 
     def zy_peer(i):
         return lax.rem(zy + i, 2 * NZ)
@@ -81,10 +80,18 @@
 
     barrier = pltpu.get_barrier_semaphore()
 
-    @pl.loop(1, 2 * NR)
+    def greet(where):
+        pl.semaphore_signal(barrier, inc=1, device_id=where, device_id_type=MESH)
+
+    @pl.loop(1, 2 * NZ)
     def _(i):
-        pl.semaphore_signal(barrier, inc=1, device_id=at_rc(rc_peer(i)), device_id_type=MESH)
-        pl.semaphore_signal(barrier, inc=1, device_id=at_zy(zy_peer(i)), device_id_type=MESH)
+        greet(at_zy(zy_peer(i)))
+
+    @pl.loop(1, NR)
+    def _(i):
+        greet(at_row(row_peer(i)))
+
+    greet(mate)
 
     @pl.loop(0, place.shape[0])
     def _(b):
@@ -97,18 +104,8 @@
         for k in range(1, structure.shape[1]):
             used = used + bits[structure[s, k]]
         seen = [lax.shift_right_logical(used, jnp.int32(i)) & 1 for i in range(slots)]
-        before = jnp.int32(0)
-        spots = []
         for i in range(slots):
             mask[s, i] = seen[i]
-            pos[s, i] = before * seen[i]
-            spots.append(before)
-            before = before + seen[i]
-        for k in range(CAP):
-            found = jnp.int32(0)
-            for i in range(slots):
-                found = found + i * seen[i] * (spots[i] == k).astype(jnp.int32)
-            ids[s, k] = found
 
     load_panel.wait()
     load_dinv.wait()
@@ -125,7 +122,7 @@
             for h in range(2):
                 nsrc[s, k // 4, (k % 4) * 2 + h] = part[:, h * lane:(h + 1) * lane]
 
-    pl.semaphore_wait(barrier, 2 * (2 * NR - 1))
+    pl.semaphore_wait(barrier, 2 * NZ - 1 + NR)
 
     def exchange_row(g):
         span = pl.ds(g * group, group)
@@ -155,6 +152,20 @@
     send(a_ref.at[:, :, 1 - core], af.at[core], a_sem.at[1], a_sem.at[2], mate)
     exchange_col(0)
 
+    @pl.loop(0, nodes)
+    def _(s):
+        before = jnp.int32(0)
+        spots = []
+        for i in range(slots):
+            pos[s, i] = before * mask[s, i]
+            spots.append(before)
+            before = before + mask[s, i]
+        for k in range(CAP):
+            found = jnp.int32(0)
+            for i in range(slots):
+                found = found + i * mask[s, i] * (spots[i] == k).astype(jnp.int32)
+            ids[s, k] = found
+
     @pl.loop(2, groups)
     def _(g):
         exchange_row(g)
@@ -167,7 +178,22 @@
     twin = {"row": other, "col": c}
     xl, xr, xo = lax.rem(x + 3, 4), lax.rem(x + 1, 4), lax.rem(x + 2, 4)
     way = 1 - 2 * core
-    onward = at_zy(lax.rem(z + way + NZ, NZ) * 2 + yh)
+    long_hops, short_hops = NZ // 2, NZ // 2 - 1
+
+    def z_at(d):
+        return lax.rem(z + d + NZ, NZ)
+
+    after_long = at_zy(z_at(-way) * 2 + yh)
+    after_short = at_zy(z_at(way) * 2 + yh)
+
+    def pass_long(s, t):
+        part = ybuf.at[s, z_at(-way * (long_hops - t))]
+        send(part, rbuf.at[s, t], ring_s.at[s, t], ring_r.at[s, t], after_long)
+
+    def pass_short(s, t):
+        part = ybuf.at[s, z_at(way * (short_hops - t))]
+        k = long_hops + t
+        send(part, rbuf.at[s, k], ring_s.at[s, k], ring_r.at[s, k], after_short)
 
     def block(s, p):
         return nbuf.at[s, p, :, core]
@@ -231,20 +257,28 @@
             rows = ahi.shape[1]
             ybuf[s, :, 2 * m] = total[:rows].reshape(NZ, 2, sub, width)
             ybuf[s, :, 2 * m + 1] = total[rows:].reshape(NZ, 2, sub, width)
-        b = lax.rem(z - way + NZ, NZ)
-        send(ybuf.at[s, b], rbuf.at[s, 0], ring_s.at[s, 0], ring_r.at[s, 0], onward)
+        pass_long(s, 0)
+        pass_short(s, 0)
         send(nboth.at[s, 0], nboth.at[s, 1], n_s.at[s], n_r.at[s], across)
 
     def ring(s, t):
         wait_for(rbuf.at[s, t], ring_r.at[s, t])
-        b = lax.rem(z - way * (t + 2) + 2 * NZ, NZ)
+        b = z_at(-way * (long_hops - 1 - t))
         ybuf[s, b] = ybuf[s, b] + rbuf[s, t]
 
-        @pl.when(t < NZ - 2)
+        @pl.when(t < long_hops - 1)
         def _():
-            send(ybuf.at[s, b], rbuf.at[s, t + 1], ring_s.at[s, t + 1], ring_r.at[s, t + 1], onward)
-
-        @pl.when(t == NZ - 2)
+            pass_long(s, t + 1)
+            k = long_hops + t
+            wait_for(rbuf.at[s, k], ring_r.at[s, k])
+            f = z_at(way * (short_hops - 1 - t))
+            ybuf[s, f] = ybuf[s, f] + rbuf[s, k]
+
+            @pl.when(t < short_hops - 1)
+            def _():
+                pass_short(s, t + 1)
+
+        @pl.when(t == long_hops - 1)
         def _():
             send(ybuf.at[s, z, :, 1 - yh], pbuf.at[s], p_s.at[s], p_r.at[s], across)
             wait_for(nboth.at[s, 1], n_r.at[s])
@@ -257,22 +291,28 @@
                 precision=HIGHEST, preferred_element_type=F32,
             )
             for h in range(2):
-                dbuf[s, :, h] = part[:, h * lane:(h + 1) * lane].reshape(NR, 4, sub, lane)
-            drow[s, rc] = dbuf[s, r, core]
-
-            @pl.loop(1, 2 * NR)
-            def _(i):
-                p = rc_peer(i)
-                send(dbuf.at[s, p // 2, lax.rem(p, 2)], drow.at[s, rc], d_s.at[s, 0], d_r.at[s, 0], at_rc(p))
+                dbuf[s, h] = part[:, h * lane:(h + 1) * lane].reshape(NR, 4, sub, lane)
+            send(dbuf.at[s, 1 - core], dmate.at[s], d_s.at[s, 4], d_r.at[s, 4], mate)
+
+    def diag_row(s):
+        wait_for(dmate.at[s], d_r.at[s, 4])
+        dsum[s] = dbuf[s, core] + dmate[s]
+        drow[s, r] = dsum[s, r]
+
+        @pl.loop(1, NR)
+        def _(i):
+            p = row_peer(i)
+            send(dsum.at[s, p], drow.at[s, r], d_s.at[s, 0], d_r.at[s, 0], at_row(p))
 
     def finish(s):
         wait_for(pbuf.at[s], p_r.at[s])
         yfin[...] = ybuf[s, z, :, yh] + pbuf[s]
         for k in range(slots):
             off[s, k] = yfin[pos[s, k]] * (-mask[s, k].astype(F32))
+        pltpu.make_async_copy(off.at[s], off_ref.at[s], o_sem.at[0, s]).start()
 
     def diag_z(s):
-        wait_for(drow.at[s, pl.ds(0, 2 * NR - 1)], d_r.at[s, 0])
+        wait_for(drow.at[s, pl.ds(0, NR - 1)], d_r.at[s, 0])
         ebuf[s] = jnp.sum(drow[s], axis=0)
         ez[s, zy] = ebuf[s, lax.rem(z, 4)]
 
@@ -284,24 +324,31 @@
     def spread_z(s):
         wait_for(ez.at[s, pl.ds(0, 2 * NZ - 1)], d_r.at[s, 1])
         u = lax.rem(z, 4)
-        gr[s, rc, u] = jnp.sum(ez[s], axis=0)
+        here = gr.at[s, core, r, u]
+        gr[s, core, r, u] = jnp.sum(ez[s], axis=0)
         for i in range(1, 4):
             t = (z // 4) * 4 + lax.rem(z + i, 4)
-            send(gr.at[s, rc, u], gr.at[s, rc, u], d_s.at[s, 2], d_r.at[s, 2], at_zy(t * 2 + yh))
+            send(here, here, d_s.at[s, 2], d_r.at[s, 2], at_zy(t * 2 + yh))
 
     def spread_row(s):
-        wait_for(gr.at[s, rc, pl.ds(0, 3)], d_r.at[s, 2])
-
-        @pl.loop(1, 2 * NR)
+        wait_for(gr.at[s, core, r, pl.ds(0, 3)], d_r.at[s, 2])
+        here = gr.at[s, core, r]
+
+        @pl.loop(1, NR)
         def _(i):
-            send(gr.at[s, rc], gr.at[s, rc], d_s.at[s, 3], d_r.at[s, 3], at_rc(rc_peer(i)))
+            send(here, here, d_s.at[s, 3], d_r.at[s, 3], at_row(row_peer(i)))
+
+    def spread_core(s):
+        wait_for(gr.at[s, core, pl.ds(0, NR - 1)], d_r.at[s, 3])
+        here = gr.at[s, core]
+        send(here, here, d_s.at[s, 5], d_r.at[s, 5], mate)
 
     def gather_diag(s):
-        wait_for(gr.at[s, pl.ds(0, 2 * NR - 1)], d_r.at[s, 3])
-        whole = gr[s].reshape(NR, 2, 4, sub, lane)
+        wait_for(gr.at[s, 1 - core], d_r.at[s, 5])
         for h in range(2):
             here = slice(h * lane, (h + 1) * lane)
-            diag[s, :, here] = lead[s, :, here] + whole[:, h].reshape(width, lane)
+            diag[s, :, here] = lead[s, :, here] + gr[s, h].reshape(width, lane)
+        pltpu.make_async_copy(diag.at[s], diag_ref.at[s], o_sem.at[1, s]).start()
 
     def leading(s):
         lead[s] = lax.dot_general(
@@ -309,21 +356,35 @@
             precision=HIGHEST, preferred_element_type=F32,
         )
 
-    last = LAG + NZ - 1
+    def settle(s):
+        wait_for(abuf.at[s, pl.ds(0, NR - 1)], s1_s.at[s])
+        wait_for(nbuf.at[pl.ds(0, group), r, pl.ds(0, 2 * NZ - 1), core], s2_s.at[s])
+        wait_for(block(s, r), c1_s.at[s])
+        for w in range(2):
+            wait_for(two(s, 0), c2_s.at[s, w])
+            wait_for(block(s, r), c3_s.at[s, w])
+        wait_for(nbuf.at[s, :, :, core], sh_s.at[s])
+        wait_for(nboth.at[s, 0], n_s.at[s])
+        for t in range(NZ - 1):
+            wait_for(rbuf.at[s, t], ring_s.at[s, t])
+        wait_for(pbuf.at[s], p_s.at[s])
+
+    last = LAG + long_hops
     stages = (
+        (2, relay_three), (1, relay_two), (0, relay_one), (3, relay_four), (LAG, multiply),
+        (last + 1, diag_row), (last + 2, diag_z), (last + 4, spread_z), (last + 5, spread_row),
+        (last + 7, spread_core), (last + 8, gather_diag),
         None,
-        (3, relay_four), (LAG, multiply), (2, relay_three), (1, relay_two), (0, relay_one),
-        (last + 8, gather_diag), (last + 6, spread_row), (last + 4, spread_z), (last + 2, diag_z),
-        (last + 3, finish), (LAG + 1, leading),
+        (last + 4, finish), (LAG + 1, leading), (last + 4, settle),
     )
 
     @pl.loop(0, nodes + last + 8)
     def _(n):
         for entry in stages:
             if entry is None:
-                @pl.loop(0, NZ - 1)
+                @pl.loop(0, long_hops)
                 def _(i):
-                    t = NZ - 2 - i
+                    t = long_hops - 1 - i
                     s = n - (LAG + 1) - t
 
                     @pl.when((s >= 0) & (s < nodes))
@@ -351,28 +412,32 @@
                     alo[k, :, h * cols:(h + 1) * cols] = low
 
     wait_for(af.at[core], a_sem.at[1])
-    for g in range(groups):
-        wait_for(abuf.at[g, pl.ds(0, NR - 1)], s1_s.at[g])
-        wait_for(nbuf.at[pl.ds(0, group), r, pl.ds(0, 2 * NZ - 1), core], s2_s.at[g])
 
     @pl.loop(0, nodes)
     def _(s):
-        wait_for(block(s, r), c1_s.at[s])
-        for w in range(2):
-            wait_for(two(s, 0), c2_s.at[s, w])
-            wait_for(block(s, r), c3_s.at[s, w])
-        wait_for(nbuf.at[s, :, :, core], sh_s.at[s])
-        wait_for(nboth.at[s, 0], n_s.at[s])
-
-        @pl.loop(0, NZ - 1)
-        def _(t):
-            wait_for(rbuf.at[s, t], ring_s.at[s, t])
-
-        wait_for(pbuf.at[s], p_s.at[s])
-        wait_for(drow.at[s, pl.ds(0, 2 * NR - 1)], d_s.at[s, 0])
+        wait_for(drow.at[s, pl.ds(0, NR - 1)], d_s.at[s, 0])
         wait_for(ez.at[s, pl.ds(0, 2 * NZ - 1)], d_s.at[s, 1])
-        wait_for(gr.at[s, rc, pl.ds(0, 3)], d_s.at[s, 2])
-        wait_for(gr.at[s, pl.ds(0, 2 * NR - 1)], d_s.at[s, 3])
+        wait_for(gr.at[s, core, r, pl.ds(0, 3)], d_s.at[s, 2])
+        wait_for(gr.at[s, core, pl.ds(0, NR - 1)], d_s.at[s, 3])
+        wait_for(dmate.at[s], d_s.at[s, 4])
+        wait_for(gr.at[s, core], d_s.at[s, 5])
+        wait_for(off.at[s], o_sem.at[0, s])
+        wait_for(diag.at[s], o_sem.at[1, s])
+
+
+def hand_over(off_ref, diag_ref, off_out, diag_out, off, diag, sems):
+    pairs = ((diag_ref, diag, diag_out), (off_ref, off, off_out))
+    pieces = diag.shape[0]
+    for k in range(pieces):
+        for i, (src, held, _) in enumerate(pairs):
+            pltpu.make_async_copy(src.at[k], held.at[k], sems.at[0, i, k]).start()
+    for k in range(pieces):
+        for i, (src, held, dst) in enumerate(pairs):
+            pltpu.make_async_copy(src.at[k], held.at[k], sems.at[0, i, k]).wait()
+            pltpu.make_async_copy(held.at[k], dst.at[k], sems.at[1, i, k]).start()
+    for k in range(pieces):
+        for i, (_, held, dst) in enumerate(pairs):
+            pltpu.make_async_copy(held.at[k], dst.at[k], sems.at[1, i, k]).wait()
 
 
 def body(ancestor_inverse, panel, diag_inverse, structure, block_slot):
@@ -383,19 +448,21 @@
     flat = slots * sub
     blocks = ancestor_inverse.reshape(slots, 2 * NZ, 2, sub, 2 * width)
     rows, depth = width // 2, 4 * width
-    vmem = pl.BlockSpec(memory_space=pltpu.VMEM)
     smem = pl.BlockSpec(memory_space=pltpu.SMEM)
     hbm = pl.BlockSpec(memory_space=pl.ANY)
     dma = pltpu.SemaphoreType.DMA
-    return pl.pallas_call(
+    shapes = (
+        jax.ShapeDtypeStruct((nodes, slots, sub, width), F32),
+        jax.ShapeDtypeStruct((nodes, width, width), F32),
+    )
+    off, diag = pl.pallas_call(
         functools.partial(kernel, group),
-        out_shape=(
-            jax.ShapeDtypeStruct((nodes, slots, sub, width), F32),
-            jax.ShapeDtypeStruct((nodes, width, width), F32),
-        ),
+        out_shape=shapes,
         in_specs=[smem, smem, hbm, hbm, hbm],
-        out_specs=(vmem, vmem),
+        out_specs=(hbm, hbm),
         scratch_shapes=[
+            pltpu.VMEM((nodes, slots, sub, width), F32),
+            pltpu.VMEM((nodes, width, width), F32),
             pltpu.SMEM(block_slot.shape, jnp.int32),
             pltpu.SMEM((nodes, CAP), jnp.int32),
             pltpu.SMEM((nodes, slots), jnp.int32),
@@ -416,13 +483,15 @@
             pltpu.VMEM((nodes, CAP, sub, width), F32),
             pltpu.VMEM((CAP, sub, width), F32),
             pltpu.VMEM((2 * flat, width), F32),
-            pltpu.VMEM((nodes, NR, 2, 4, sub, lane), F32),
-            pltpu.VMEM((nodes, 2 * NR, 4, sub, lane), F32),
+            pltpu.VMEM((nodes, 2, NR, 4, sub, lane), F32),
+            pltpu.VMEM((nodes, NR, 4, sub, lane), F32),
+            pltpu.VMEM((nodes, NR, 4, sub, lane), F32),
+            pltpu.VMEM((nodes, NR, 4, sub, lane), F32),
             pltpu.VMEM((nodes, 4, sub, lane), F32),
             pltpu.VMEM((nodes, 2 * NZ, sub, lane), F32),
-            pltpu.VMEM((nodes, 2 * NR, 4, sub, lane), F32),
+            pltpu.VMEM((nodes, 2, NR, 4, sub, lane), F32),
             pltpu.VMEM((nodes, width, width), F32),
-            dma((2,)), dma((3,)),
+            dma((2,)), dma((2, nodes)), dma((3,)),
             dma((groups,)), dma((groups,)), dma((groups,)),
             dma((groups,)), dma((groups,)), dma((groups,)),
             dma((nodes,)), dma((nodes,)),
@@ -432,13 +501,23 @@
             dma((nodes,)), dma((nodes,)),
             dma((nodes, NZ - 1)), dma((nodes, NZ - 1)),
             dma((nodes,)), dma((nodes,)),
-            dma((nodes, 4)), dma((nodes, 4)),
+            dma((nodes, 6)), dma((nodes, 6)),
         ],
         compiler_params=pltpu.CompilerParams(
             collective_id=0, has_side_effects=True, vmem_limit_bytes=62 * 1024 * 1024
         ),
         name="invert_level",
     )(structure, block_slot, blocks, panel, diag_inverse)
+    return pl.pallas_call(
+        hand_over,
+        out_shape=shapes,
+        in_specs=[hbm, hbm],
+        out_specs=(hbm, hbm),
+        scratch_shapes=[
+            pltpu.VMEM(off.shape, F32), pltpu.VMEM(diag.shape, F32), dma((2, 2, nodes)),
+        ],
+        name="hand_over",
+    )(off, diag)
 
 
 def solution(mesh):

time: 140 us -> 125 us (0.89)
  Pallas kernels: 135 us -> 124 us
  local copies, waits for them, and re-layouts: 4.51 us -> 0 us
    pallas_call x1 -> x2, Pallas kernels: 135 us -> 124 us  [the longest x1 121 us: body(): pl.pallas_call(functools.partial(kernel, group), out_shape=shapes, in_spe...]
    unnamed x2 -> x0, local copies, waits for them, and re-layouts: 4.51 us -> none
where the time goes in v4:
time: 125 us; the launch traced here: 124 us
  Pallas kernels  124 us (99%)
    pallas_call x1, Pallas kernels, body(): pl.pallas_call(functools.partial(kernel, group), out_shape=shapes, in_spe...  121 us

profile of v4, /device:TPU:1, one launch (start us, length us, event | category | flops | bytes accessed | tf_op | source)
XLA Modules:
  0.0 124.5 jit_solution(14085785810221559136)
XLA Ops:
  0.6 121.4 %invert_level.1 = (f32[6,8,8,256]{3,2,1,0:T(8,128)}, f32[6,256,256]{2,1,0:T(8,128)}) custom-call(s32[6,32]{1,0:T(8,128)} %structure.1, s32[64]{0:T(128)} %place.1, f32[8,16,2,8,512]{4,3,2,1,0:T(8,128)} %bitcast.1, f32[6,8,8,256]{3,2,1,0:T(8,128)} %panel_ref.1, f32[6,256,256]{2,1,0:T(8,128)} %dinv_ref.1), custom_call_target="tpu_custom_call" | custom-call | tf_op jit(solution)/shard_map/invert_level/pallas_call | solution.py:458
  122.1 2.4 %hand_over.1 = (f32[6,8,8,256]{3,2,1,0:T(8,128)}, f32[6,256,256]{2,1,0:T(8,128)}) custom-call(f32[6,8,8,256]{3,2,1,0:T(8,128)} %get-tuple-element.4.off_ref, f32[6,256,256]{2,1,0:T(8,128)} %get-tuple-element.5.diag_ref), custom_call_target="tpu_custom_call" | custom-call | tf_op jit(solution)/shard_map/hand_over/pallas_call | solution.py:511

commit v5 on v4

--- a/solution.py
+++ b/solution.py
@@ -62,6 +62,14 @@
     def at_zy(t):
         return {"row": r, "col": t * 2 + core}
 
+    plane = r * 2 + yh
+
+    def at_plane(t):
+        return {"row": t // 2, "col": (z * 2 + lax.rem(t, 2)) * 2 + core}
+
+    def plane_peer(i):
+        return lax.rem(plane + i, 2 * NR)
+
     def row_peer(i):
         return lax.rem(r + i, NR)
 
@@ -90,6 +98,7 @@
     @pl.loop(1, NR)
     def _(i):
         greet(at_row(row_peer(i)))
+        greet(at_plane(row_peer(i) * 2 + 1 - yh))
 
     greet(mate)
 
@@ -122,7 +131,7 @@
             for h in range(2):
                 nsrc[s, k // 4, (k % 4) * 2 + h] = part[:, h * lane:(h + 1) * lane]
 
-    pl.semaphore_wait(barrier, 2 * NZ - 1 + NR)
+    pl.semaphore_wait(barrier, 2 * NZ - 1 + 2 * NR - 1)
 
     def exchange_row(g):
         span = pl.ds(g * group, group)
@@ -297,12 +306,13 @@
     def diag_row(s):
         wait_for(dmate.at[s], d_r.at[s, 4])
         dsum[s] = dbuf[s, core] + dmate[s]
-        drow[s, r] = dsum[s, r]
-
-        @pl.loop(1, NR)
+        drow[s, plane] = dsum[s, r, pl.ds(2 * yh, 2)]
+
+        @pl.loop(1, 2 * NR)
         def _(i):
-            p = row_peer(i)
-            send(dsum.at[s, p], drow.at[s, r], d_s.at[s, 0], d_r.at[s, 0], at_row(p))
+            p = plane_peer(i)
+            mine = dsum.at[s, p // 2, pl.ds(2 * lax.rem(p, 2), 2)]
+            send(mine, drow.at[s, plane], d_s.at[s, 0], d_r.at[s, 0], at_plane(p))
 
     def finish(s):
         wait_for(pbuf.at[s], p_r.at[s])
@@ -312,34 +322,34 @@
         pltpu.make_async_copy(off.at[s], off_ref.at[s], o_sem.at[0, s]).start()
 
     def diag_z(s):
-        wait_for(drow.at[s, pl.ds(0, NR - 1)], d_r.at[s, 0])
+        wait_for(drow.at[s, pl.ds(0, 2 * NR - 1)], d_r.at[s, 0])
         ebuf[s] = jnp.sum(drow[s], axis=0)
-        ez[s, zy] = ebuf[s, lax.rem(z, 4)]
-
-        @pl.loop(1, 2 * NZ)
+        ez[s, z] = ebuf[s, lax.rem(z, 2)]
+
+        @pl.loop(1, NZ)
         def _(i):
-            t = zy_peer(i)
-            send(ebuf.at[s, lax.rem(t // 2, 4)], ez.at[s, zy], d_s.at[s, 1], d_r.at[s, 1], at_zy(t))
+            t = lax.rem(z + i, NZ)
+            send(ebuf.at[s, lax.rem(t, 2)], ez.at[s, z], d_s.at[s, 1], d_r.at[s, 1], at_zy(t * 2 + yh))
+
+    tile = r * 4 + yh * 2
 
     def spread_z(s):
-        wait_for(ez.at[s, pl.ds(0, 2 * NZ - 1)], d_r.at[s, 1])
-        u = lax.rem(z, 4)
-        here = gr.at[s, core, r, u]
-        gr[s, core, r, u] = jnp.sum(ez[s], axis=0)
-        for i in range(1, 4):
-            t = (z // 4) * 4 + lax.rem(z + i, 4)
-            send(here, here, d_s.at[s, 2], d_r.at[s, 2], at_zy(t * 2 + yh))
+        wait_for(ez.at[s, pl.ds(0, NZ - 1)], d_r.at[s, 1])
+        u = tile + lax.rem(z, 2)
+        here = gr.at[s, core, u]
+        gr[s, core, u] = jnp.sum(ez[s], axis=0)
+        send(here, here, d_s.at[s, 2], d_r.at[s, 2], at_zy((z + 1 - 2 * lax.rem(z, 2)) * 2 + yh))
 
     def spread_row(s):
-        wait_for(gr.at[s, core, r, pl.ds(0, 3)], d_r.at[s, 2])
-        here = gr.at[s, core, r]
-
-        @pl.loop(1, NR)
+        wait_for(gr.at[s, core, tile], d_r.at[s, 2])
+        here = gr.at[s, core, pl.ds(tile, 2)]
+
+        @pl.loop(1, 2 * NR)
         def _(i):
-            send(here, here, d_s.at[s, 3], d_r.at[s, 3], at_row(row_peer(i)))
+            send(here, here, d_s.at[s, 3], d_r.at[s, 3], at_plane(plane_peer(i)))
 
     def spread_core(s):
-        wait_for(gr.at[s, core, pl.ds(0, NR - 1)], d_r.at[s, 3])
+        wait_for(gr.at[s, core, pl.ds(0, 4 * NR - 2)], d_r.at[s, 3])
         here = gr.at[s, core]
         send(here, here, d_s.at[s, 5], d_r.at[s, 5], mate)
 
@@ -415,10 +425,10 @@
 
     @pl.loop(0, nodes)
     def _(s):
-        wait_for(drow.at[s, pl.ds(0, NR - 1)], d_s.at[s, 0])
-        wait_for(ez.at[s, pl.ds(0, 2 * NZ - 1)], d_s.at[s, 1])
-        wait_for(gr.at[s, core, r, pl.ds(0, 3)], d_s.at[s, 2])
-        wait_for(gr.at[s, core, pl.ds(0, NR - 1)], d_s.at[s, 3])
+        wait_for(drow.at[s, pl.ds(0, 2 * NR - 1)], d_s.at[s, 0])
+        wait_for(ez.at[s, pl.ds(0, NZ - 1)], d_s.at[s, 1])
+        wait_for(gr.at[s, core, tile], d_s.at[s, 2])
+        wait_for(gr.at[s, core, pl.ds(0, 4 * NR - 2)], d_s.at[s, 3])
         wait_for(dmate.at[s], d_s.at[s, 4])
         wait_for(gr.at[s, core], d_s.at[s, 5])
         wait_for(off.at[s], o_sem.at[0, s])
@@ -486,10 +496,10 @@
             pltpu.VMEM((nodes, 2, NR, 4, sub, lane), F32),
             pltpu.VMEM((nodes, NR, 4, sub, lane), F32),
             pltpu.VMEM((nodes, NR, 4, sub, lane), F32),
-            pltpu.VMEM((nodes, NR, 4, sub, lane), F32),
-            pltpu.VMEM((nodes, 4, sub, lane), F32),
-            pltpu.VMEM((nodes, 2 * NZ, sub, lane), F32),
-            pltpu.VMEM((nodes, 2, NR, 4, sub, lane), F32),
+            pltpu.VMEM((nodes, 2 * NR, 2, sub, lane), F32),
+            pltpu.VMEM((nodes, 2, sub, lane), F32),
+            pltpu.VMEM((nodes, NZ, sub, lane), F32),
+            pltpu.VMEM((nodes, 2, 4 * NR, sub, lane), F32),
             pltpu.VMEM((nodes, width, width), F32),
             dma((2,)), dma((2, nodes)), dma((3,)),
             dma((groups,)), dma((groups,)), dma((groups,)),

time: 125 us -> 122 us (0.976)
  Pallas kernels: 124 us -> 121 us
    pallas_call x1, Pallas kernels: 121 us -> 119 us  [body(): pl.pallas_call(functools.partial(kernel, group), out_shape=shapes, in_spe...]
where the time goes in v5:
time: 122 us
  Pallas kernels  121 us (99%)
    pallas_call x1, Pallas kernels, body(): pl.pallas_call(functools.partial(kernel, group), out_shape=shapes, in_spe...  119 us

profile of v5, /device:TPU:1, one launch (start us, length us, event | category | flops | bytes accessed | tf_op | source)
XLA Modules:
  0.0 121.8 jit_solution(3105066631173113764)
XLA Ops:
  0.6 118.7 %invert_level.1 = (f32[6,8,8,256]{3,2,1,0:T(8,128)}, f32[6,256,256]{2,1,0:T(8,128)}) custom-call(s32[6,32]{1,0:T(8,128)} %structure.1, s32[64]{0:T(128)} %place.1, f32[8,16,2,8,512]{4,3,2,1,0:T(8,128)} %bitcast.1, f32[6,8,8,256]{3,2,1,0:T(8,128)} %panel_ref.1, f32[6,256,256]{2,1,0:T(8,128)} %dinv_ref.1), custom_call_target="tpu_custom_call" | custom-call | tf_op jit(solution)/shard_map/invert_level/pallas_call | solution.py:468
  119.4 2.4 %hand_over.1 = (f32[6,8,8,256]{3,2,1,0:T(8,128)}, f32[6,256,256]{2,1,0:T(8,128)}) custom-call(f32[6,8,8,256]{3,2,1,0:T(8,128)} %get-tuple-element.4.off_ref, f32[6,256,256]{2,1,0:T(8,128)} %get-tuple-element.5.diag_ref), custom_call_target="tpu_custom_call" | custom-call | tf_op jit(solution)/shard_map/hand_over/pallas_call | solution.py:521

commit v6 on v5

--- a/solution.py
+++ b/solution.py
@@ -29,11 +29,11 @@
 
 def kernel(
     group,
-    structure, place, a_ref, panel_ref, dinv_ref, off_ref, diag_ref,
-    off, diag, bits, ids, pos, mask, panel, dinv,
+    structure, place, a_ref, panel_ref, dinv_ref, off, diag,
+    bits, ids, pos, mask, panel, dinv,
     af, ahi, alo, nsrc, nboth, abuf, nbuf, nhi, nlo, ybuf, rbuf, pbuf, yfin, fexp,
     dbuf, dmate, dsum, drow, ebuf, ez, gr, lead,
-    in_sem, o_sem, a_sem, s1_s, s1_r, s1_l, s2_s, s2_r, s2_l,
+    in_sem, a_sem, s1_s, s1_r, s1_l, s2_s, s2_r, s2_l,
     c1_s, c1_r, c2_s, c2_r, c3_s, c3_r, sh_s, sh_r, n_s, n_r,
     ring_s, ring_r, p_s, p_r, d_s, d_r,
 ):
@@ -102,25 +102,19 @@
 
     greet(mate)
 
-    @pl.loop(0, place.shape[0])
-    def _(b):
-        slot = place[b] - r * slots
-        bits[b] = sum((slot == i).astype(jnp.int32) * (1 << i) for i in range(slots))
-
-    @pl.loop(0, nodes)
-    def _(s):
-        used = bits[structure[s, 0]]
+    for i in range(bits.shape[0]):
+        bits[i] = jnp.int32(0)
+    for i in range(slots):
+        bits[r * slots + i] = jnp.int32(1 << i)
+
+    def mark(s):
+        used = bits[place[structure[s, 0]]]
         for k in range(1, structure.shape[1]):
-            used = used + bits[structure[s, k]]
-        seen = [lax.shift_right_logical(used, jnp.int32(i)) & 1 for i in range(slots)]
+            used = used + bits[place[structure[s, k]]]
         for i in range(slots):
-            mask[s, i] = seen[i]
-
-    load_panel.wait()
-    load_dinv.wait()
-
-    @pl.loop(0, nodes)
-    def _(s):
+            mask[s, i] = lax.shift_right_logical(used, jnp.int32(i)) & 1
+
+    def normalize(s):
         value = jnp.dot(
             panel[s].reshape(flat, width), dinv[s],
             precision=HIGHEST, preferred_element_type=F32,
@@ -131,6 +125,10 @@
             for h in range(2):
                 nsrc[s, k // 4, (k % 4) * 2 + h] = part[:, h * lane:(h + 1) * lane]
 
+    mark(0)
+    load_panel.wait()
+    load_dinv.wait()
+    normalize(0)
     pl.semaphore_wait(barrier, 2 * NZ - 1 + 2 * NR - 1)
 
     def exchange_row(g):
@@ -157,8 +155,16 @@
             )
 
     exchange_row(0)
+    mark(1)
+    normalize(1)
     exchange_row(1)
     send(a_ref.at[:, :, 1 - core], af.at[core], a_sem.at[1], a_sem.at[2], mate)
+
+    @pl.loop(2, nodes)
+    def _(s):
+        mark(s)
+        normalize(s)
+
     exchange_col(0)
 
     @pl.loop(0, nodes)
@@ -319,7 +325,6 @@
         yfin[...] = ybuf[s, z, :, yh] + pbuf[s]
         for k in range(slots):
             off[s, k] = yfin[pos[s, k]] * (-mask[s, k].astype(F32))
-        pltpu.make_async_copy(off.at[s], off_ref.at[s], o_sem.at[0, s]).start()
 
     def diag_z(s):
         wait_for(drow.at[s, pl.ds(0, 2 * NR - 1)], d_r.at[s, 0])
@@ -358,7 +363,6 @@
         for h in range(2):
             here = slice(h * lane, (h + 1) * lane)
             diag[s, :, here] = lead[s, :, here] + gr[s, h].reshape(width, lane)
-        pltpu.make_async_copy(diag.at[s], diag_ref.at[s], o_sem.at[1, s]).start()
 
     def leading(s):
         lead[s] = lax.dot_general(
@@ -431,23 +435,6 @@
         wait_for(gr.at[s, core, pl.ds(0, 4 * NR - 2)], d_s.at[s, 3])
         wait_for(dmate.at[s], d_s.at[s, 4])
         wait_for(gr.at[s, core], d_s.at[s, 5])
-        wait_for(off.at[s], o_sem.at[0, s])
-        wait_for(diag.at[s], o_sem.at[1, s])
-
-
-def hand_over(off_ref, diag_ref, off_out, diag_out, off, diag, sems):
-    pairs = ((diag_ref, diag, diag_out), (off_ref, off, off_out))
-    pieces = diag.shape[0]
-    for k in range(pieces):
-        for i, (src, held, _) in enumerate(pairs):
-            pltpu.make_async_copy(src.at[k], held.at[k], sems.at[0, i, k]).start()
-    for k in range(pieces):
-        for i, (src, held, dst) in enumerate(pairs):
-            pltpu.make_async_copy(src.at[k], held.at[k], sems.at[0, i, k]).wait()
-            pltpu.make_async_copy(held.at[k], dst.at[k], sems.at[1, i, k]).start()
-    for k in range(pieces):
-        for i, (_, held, dst) in enumerate(pairs):
-            pltpu.make_async_copy(held.at[k], dst.at[k], sems.at[1, i, k]).wait()
 
 
 def body(ancestor_inverse, panel, diag_inverse, structure, block_slot):
@@ -460,6 +447,7 @@
     rows, depth = width // 2, 4 * width
     smem = pl.BlockSpec(memory_space=pltpu.SMEM)
     hbm = pl.BlockSpec(memory_space=pl.ANY)
+    vmem = pl.BlockSpec(memory_space=pltpu.VMEM)
     dma = pltpu.SemaphoreType.DMA
     shapes = (
         jax.ShapeDtypeStruct((nodes, slots, sub, width), F32),
@@ -467,12 +455,10 @@
     )
     off, diag = pl.pallas_call(
         functools.partial(kernel, group),
-        out_shape=shapes,
+        out_shape=tuple(pltpu.VMEM(a.shape, F32) for a in shapes),
         in_specs=[smem, smem, hbm, hbm, hbm],
-        out_specs=(hbm, hbm),
+        out_specs=(vmem, vmem),
         scratch_shapes=[
-            pltpu.VMEM((nodes, slots, sub, width), F32),
-            pltpu.VMEM((nodes, width, width), F32),
             pltpu.SMEM(block_slot.shape, jnp.int32),
             pltpu.SMEM((nodes, CAP), jnp.int32),
             pltpu.SMEM((nodes, slots), jnp.int32),
@@ -501,7 +487,7 @@
             pltpu.VMEM((nodes, NZ, sub, lane), F32),
             pltpu.VMEM((nodes, 2, 4 * NR, sub, lane), F32),
             pltpu.VMEM((nodes, width, width), F32),
-            dma((2,)), dma((2, nodes)), dma((3,)),
+            dma((2,)), dma((3,)),
             dma((groups,)), dma((groups,)), dma((groups,)),
             dma((groups,)), dma((groups,)), dma((groups,)),
             dma((nodes,)), dma((nodes,)),
@@ -514,20 +500,11 @@
             dma((nodes, 6)), dma((nodes, 6)),
         ],
         compiler_params=pltpu.CompilerParams(
-            collective_id=0, has_side_effects=True, vmem_limit_bytes=62 * 1024 * 1024
+            collective_id=0, has_side_effects=True, vmem_limit_bytes=61 * 1024 * 1024
         ),
         name="invert_level",
     )(structure, block_slot, blocks, panel, diag_inverse)
-    return pl.pallas_call(
-        hand_over,
-        out_shape=shapes,
-        in_specs=[hbm, hbm],
-        out_specs=(hbm, hbm),
-        scratch_shapes=[
-            pltpu.VMEM(off.shape, F32), pltpu.VMEM(diag.shape, F32), dma((2, 2, nodes)),
-        ],
-        name="hand_over",
-    )(off, diag)
+    return off, diag
 
 
 def solution(mesh):

time: 122 us -> 120 us (0.984)
  Pallas kernels: 121 us -> 118 us
  local copies, waits for them, and re-layouts: 0 us -> 1.89 us
    pallas_call x2 -> x1, Pallas kernels: 121 us -> 118 us  [body(): pl.pallas_call(functools.partial(kernel, group), out_shape=tuple((pltpu.V...]
    unnamed x0 -> x2, local copies, waits for them, and re-layouts: none -> 1.89 us
where the time goes in v6:
time: 120 us
  Pallas kernels  118 us (98%)
  local copies, waits for them, and re-layouts  1.89 us (2%)
    pallas_call x1, Pallas kernels, body(): pl.pallas_call(functools.partial(kernel, group), out_shape=tuple((pltpu.V...  118 us

profile of v6, /device:TPU:1, one launch (start us, length us, event | category | flops | bytes accessed | tf_op | source)
XLA Modules:
  0.0 120.3 jit_solution(11645205617344359048)
XLA Ops:
  0.6 117.7 %invert_level.1 = (f32[6,8,8,256]{3,2,1,0:T(8,128)S(1)}, f32[6,256,256]{2,1,0:T(8,128)S(1)}) custom-call(s32[6,32]{1,0:T(8,128)} %structure.1, s32[64]{0:T(128)} %place.1, f32[8,16,2,8,512]{4,3,2,1,0:T(8,128)} %bitcast.1, f32[6,8,8,256]{3,2,1,0:T(8,128)} %panel_ref.1, f32[6,256,256]{2,1,0:T(8,128)} %dinv_ref.1), custom_call_target="tpu_custom_call" | custom-call | tf_op jit(solution)/shard_map/invert_level/pallas_call | solution.py:456
  118.4 0.7 copy.9
  119.1 1.1 copy.10

commit v7 on v6

--- a/solution.py
+++ b/solution.py
@@ -67,8 +67,14 @@
     def at_plane(t):
         return {"row": t // 2, "col": (z * 2 + lax.rem(t, 2)) * 2 + core}
 
-    def plane_peer(i):
-        return lax.rem(plane + i, 2 * NR)
+    plane_peers = [
+        lax.rem(r // 2 + dx, 4) * 4 + (lax.rem(r, 2) if dl == 0 else 1 - lax.rem(r, 2)) * 2 + (yh if dh == 0 else 1 - yh)
+        for dx, dl, dh in sorted(
+            ((dx, dl, dh) for dx in range(4) for dl in range(2) for dh in range(2) if dx or dl or dh),
+            key=lambda d: -min(d[0], 4 - d[0]) - (1 if d[1] else 2 * d[2]),
+        )
+    ]
+    z_steps = (4, 3, 5, 2, 6, 1, 7)
 
     def row_peer(i):
         return lax.rem(r + i, NR)
@@ -314,9 +320,7 @@
         dsum[s] = dbuf[s, core] + dmate[s]
         drow[s, plane] = dsum[s, r, pl.ds(2 * yh, 2)]
 
-        @pl.loop(1, 2 * NR)
-        def _(i):
-            p = plane_peer(i)
+        for p in plane_peers:
             mine = dsum.at[s, p // 2, pl.ds(2 * lax.rem(p, 2), 2)]
             send(mine, drow.at[s, plane], d_s.at[s, 0], d_r.at[s, 0], at_plane(p))
 
@@ -331,8 +335,7 @@
         ebuf[s] = jnp.sum(drow[s], axis=0)
         ez[s, z] = ebuf[s, lax.rem(z, 2)]
 
-        @pl.loop(1, NZ)
-        def _(i):
+        for i in z_steps:
             t = lax.rem(z + i, NZ)
             send(ebuf.at[s, lax.rem(t, 2)], ez.at[s, z], d_s.at[s, 1], d_r.at[s, 1], at_zy(t * 2 + yh))
 
@@ -349,14 +352,18 @@
         wait_for(gr.at[s, core, tile], d_r.at[s, 2])
         here = gr.at[s, core, pl.ds(tile, 2)]
 
-        @pl.loop(1, 2 * NR)
-        def _(i):
-            send(here, here, d_s.at[s, 3], d_r.at[s, 3], at_plane(plane_peer(i)))
+        for p in plane_peers:
+            send(here, here, d_s.at[s, 3], d_r.at[s, 3], at_plane(p))
 
     def spread_core(s):
         wait_for(gr.at[s, core, pl.ds(0, 4 * NR - 2)], d_r.at[s, 3])
         here = gr.at[s, core]
         send(here, here, d_s.at[s, 5], d_r.at[s, 5], mate)
+        wait_for(drow.at[s, pl.ds(0, 2 * NR - 1)], d_s.at[s, 0])
+        wait_for(ez.at[s, pl.ds(0, NZ - 1)], d_s.at[s, 1])
+        wait_for(gr.at[s, core, tile], d_s.at[s, 2])
+        wait_for(dmate.at[s], d_s.at[s, 4])
+        wait_for(gr.at[s, core, pl.ds(0, 4 * NR - 2)], d_s.at[s, 3])
 
     def gather_diag(s):
         wait_for(gr.at[s, 1 - core], d_r.at[s, 5])
@@ -385,11 +392,11 @@
 
     last = LAG + long_hops
     stages = (
-        (2, relay_three), (1, relay_two), (0, relay_one), (3, relay_four), (LAG, multiply),
+        (2, relay_three), (1, relay_two), (0, relay_one), (3, relay_four), (LAG + 1, leading), (LAG, multiply),
         (last + 1, diag_row), (last + 2, diag_z), (last + 4, spread_z), (last + 5, spread_row),
         (last + 7, spread_core), (last + 8, gather_diag),
         None,
-        (last + 4, finish), (LAG + 1, leading), (last + 4, settle),
+        (last + 4, finish), (last + 4, settle),
     )
 
     @pl.loop(0, nodes + last + 8)
@@ -429,11 +436,6 @@
 
     @pl.loop(0, nodes)
     def _(s):
-        wait_for(drow.at[s, pl.ds(0, 2 * NR - 1)], d_s.at[s, 0])
-        wait_for(ez.at[s, pl.ds(0, NZ - 1)], d_s.at[s, 1])
-        wait_for(gr.at[s, core, tile], d_s.at[s, 2])
-        wait_for(gr.at[s, core, pl.ds(0, 4 * NR - 2)], d_s.at[s, 3])
-        wait_for(dmate.at[s], d_s.at[s, 4])
         wait_for(gr.at[s, core], d_s.at[s, 5])
 
 

time: 120 us -> 120 us (level)
  no operation moved by 1% of the time
where the time goes in v7:
time: 120 us
  Pallas kernels  117 us (98%)
  local copies, waits for them, and re-layouts  1.89 us (2%)
    pallas_call x1, Pallas kernels, body(): pl.pallas_call(functools.partial(kernel, group), out_shape=tuple((pltpu.V...  117 us

profile of v7, /device:TPU:1, one launch (start us, length us, event | category | flops | bytes accessed | tf_op | source)
XLA Modules:
  0.0 119.7 jit_solution(7601779853838720535)
XLA Ops:
  0.6 117.2 %invert_level.1 = (f32[6,8,8,256]{3,2,1,0:T(8,128)S(1)}, f32[6,256,256]{2,1,0:T(8,128)S(1)}) custom-call(s32[6,32]{1,0:T(8,128)} %structure.1, s32[64]{0:T(128)} %place.1, f32[8,16,2,8,512]{4,3,2,1,0:T(8,128)} %bitcast.1, f32[6,8,8,256]{3,2,1,0:T(8,128)} %panel_ref.1, f32[6,256,256]{2,1,0:T(8,128)} %dinv_ref.1), custom_call_target="tpu_custom_call" | custom-call | tf_op jit(solution)/shard_map/invert_level/pallas_call | solution.py:458
  117.8 0.7 copy.9
  118.6 1.1 copy.10
